TPU v7x, 32 devices: a whole 2x2x4 slice. The times are simulated.
32 devices in a mesh: gx: 8 (over y, x, core), gy: 4 (over z).
Axes of the slice: x: 2, y: 2, z: 4, core: 2. Of those that a mesh axis runs over, the one named last changes fastest.
Arguments:
- state: float32 [4, 64, 2, 16, 512], P(None, None, None, 'gx', 'gy'), may hold values from -6 to 6
- register: float32 [4, 64, 2, 16, 512], P(None, None, None, 'gx', 'gy'), may hold values from -6 to 6
- cotangent: float32 [4, 64, 2, 16, 512], P(None, None, None, 'gx', 'gy'), may hold values from -6 to 6
- impedance: float32 [2048], P('gy'), may hold values from 0.2 to 5
- wall_patch: int32 [2, 16, 512], P(None, 'gx', 'gy'), may hold values from 0 to 2047
Outputs:
- next_state: float32 [4, 64, 2, 16, 512], P(None, None, None, 'gx', 'gy')
- next_register: float32 [4, 64, 2, 16, 512], P(None, None, None, 'gx', 'gy')
- state_gradient: float32 [4, 64, 2, 16, 512], P(None, None, None, 'gx', 'gy')
- impedance_gradient: float32 [2048], P('gy')
All inputs are finite; a program needn't handle non-finite values.
Results may differ from a plain program's by a relative error of at most 0.00014.
Values sent between devices are 32-bit elements; how exact they have to be, the bound alone decides.
No kernel may reach another device: no remote copies, remote signals or barrier semaphores. Data moves between devices by JAX's collectives and lax.ppermute only.
A program may use at most 64 MiB of HBM per device.

v0:
```python
import functools
import math

import jax
import jax.numpy as jnp
import numpy as np
from jax import lax
from jax.experimental import pallas as pl
from jax.experimental.pallas import tpu as pltpu
from jax.sharding import PartitionSpec as P

time_step = 0.02
section_a = -0.4178904745
section_b = 0.3792103129
lift_half = 6.0

LANES = 128
HALO_LANES = 48
IMP_LANE = 48
SUM_LANE = 64


def derivative_table():
    points = np.array([-1.0, -1.0 / math.sqrt(5.0), 1.0 / math.sqrt(5.0), 1.0])
    identity = np.eye(4)
    distance = points[:, None] - points[None, :] + identity
    barycentric = 1.0 / np.prod(distance, axis=1)
    matrix = barycentric[None, :] / (barycentric[:, None] * distance)
    matrix = matrix * (1.0 - identity)
    matrix = matrix - identity * matrix.sum(axis=1)[:, None]
    return 2.0 * matrix


def row_of(field, a, b, half):
    return field * 256 + a * 64 + b * 16 + half * 8


def load(ref, field, a, b, half):
    return ref[pl.ds(row_of(field, a, b, half), 8), :]


def sub_roll(value, shift):
    return pltpu.roll(value, shift % 8, 0)


def lane_roll(value, shift):
    shift = shift % LANES
    return value if shift == 0 else pltpu.roll(value, shift, 1)


def rows_iota():
    return lax.broadcasted_iota(jnp.int32, (8, LANES), 0)


def lanes_iota():
    return lax.broadcasted_iota(jnp.int32, (8, LANES), 1)


def x_trace(ref, sigma, a, b, half):
    flip = sigma if a == 3 else -sigma
    press, normal = load(ref, 0, a, b, half), load(ref, 1, a, b, half)
    mixed = press + normal if flip > 0 else press - normal
    return [mixed, load(ref, 2, a, b, half), load(ref, 3, a, b, half)]


def y_trace(ref, sigma, a, b, half):
    flip = sigma if b == 3 else -sigma
    press, normal = load(ref, 0, a, b, half), load(ref, 2, a, b, half)
    mixed = press + normal if flip > 0 else press - normal
    return [mixed, load(ref, 1, a, b, half), load(ref, 3, a, b, half)]


def pack_kernel(gx, gy, st, ct, imp, wp, first, second, chunks):
    me_x, me_y = lax.axis_index("gx"), lax.axis_index("gy")
    rows, lanes = rows_iota(), lanes_iota()
    even_row = (rows & 1) == 0
    even_me = (me_x & 1) == 0
    for number, (ref, sigma) in enumerate(((st, 1), (ct, -1))):
        for b in range(4):
            high = [x_trace(ref, sigma, 3, b, half) for half in range(2)]
            low = [x_trace(ref, sigma, 0, b, half) for half in range(2)]
            for part in range(3):
                to_right = jnp.where(even_row, sub_roll(high[0][part], -1), high[1][part])
                to_left = jnp.where(even_row, low[1][part], sub_roll(low[0][part], 1))
                at = pl.ds(((number * 3 + part) * 4 + b) * 8, 8)
                first[at, :] = jnp.where(even_me, to_right, to_left)
                second[at, :] = jnp.where(even_me, to_left, to_right)
    up = jnp.zeros((8, LANES), jnp.float32)
    down = jnp.zeros((8, LANES), jnp.float32)
    for number, (ref, sigma) in enumerate(((st, 1), (ct, -1))):
        for a in range(4):
            for half in range(2):
                high = y_trace(ref, sigma, a, 3, half)
                low = y_trace(ref, sigma, a, 0, half)
                for part in range(3):
                    k = (number * 3 + part) * 8 + a * 2 + half
                    up = jnp.where(lanes == k, lane_roll(high[part], k - 127), up)
                    down = jnp.where(lanes == k, lane_roll(low[part], k), down)
    floor = jnp.zeros((8, LANES), jnp.float32)
    ceil = jnp.zeros((8, LANES), jnp.float32)
    for a in range(4):
        for b in range(4):
            floor += (load(st, 0, a, b, 0) - load(st, 3, a, b, 0)) * (
                load(ct, 0, a, b, 0) + load(ct, 3, a, b, 0)
            )
            ceil += (load(st, 0, a, b, 1) + load(st, 3, a, b, 1)) * (
                load(ct, 0, a, b, 1) - load(ct, 3, a, b, 1)
            )
    values = jnp.concatenate([floor[0:1], floor[1:2], ceil[6:7], ceil[7:8]], axis=1)
    patch = jnp.concatenate([wp[r : r + 1, :] for r in range(4)], axis=1)
    groups = 4 * gy
    count = 4 * LANES
    high_of = lax.shift_right_logical(patch, 7)
    low_of = patch & (LANES - 1)
    chosen = lax.broadcasted_iota(jnp.int32, (groups, count), 0) == high_of
    spread = jnp.where(chosen, jnp.broadcast_to(values, (groups, count)), 0.0)
    top = spread.astype(jnp.bfloat16)
    rest = spread - top.astype(jnp.float32)
    middle = rest.astype(jnp.bfloat16)
    last = (rest - middle.astype(jnp.float32)).astype(jnp.bfloat16)
    pieces = jnp.concatenate([top, middle, last], axis=0)
    hot = lax.broadcasted_iota(jnp.int32, (LANES, count), 0) == low_of
    hot = jnp.where(hot, 1.0, 0.0).astype(jnp.bfloat16)
    sums = lax.dot_general(
        pieces, hot, (((1,), (1,)), ((), ())), preferred_element_type=jnp.float32
    )
    sums = sums[:groups] + sums[groups : 2 * groups] + sums[2 * groups :]
    width = LANES // gx
    shard = jnp.concatenate([imp[...], imp[...]], axis=0)
    placed = pltpu.roll(shard, (IMP_LANE - me_x * width + LANES) % LANES, 1)
    odd_me_y = me_y & 1
    imp_here = (
        (lanes >= IMP_LANE)
        & (lanes < IMP_LANE + width)
        & (lax.shift_right_logical(rows, 2) == odd_me_y)
    )
    common = jnp.where(imp_here, placed, 0.0)
    upper_lanes = lanes >= SUM_LANE
    tiles = []
    for target in range(gy):
        part = sums[target * 4 : target * 4 + 4]
        both = jnp.concatenate([pltpu.roll(part, SUM_LANE, 1), part], axis=0)
        tiles.append(jnp.where(upper_lanes, both, common))
    for x in range(gx):
        for target in range(gy):
            chunks[x * gy + target] = tiles[target]
    halo_lanes = lanes < HALO_LANES
    next_y = me_x * gy + lax.rem(me_y + 1, gy)
    prev_y = me_x * gy + lax.rem(me_y + gy - 1, gy)
    chunks[next_y] = jnp.where(halo_lanes, up, chunks[next_y])
    chunks[prev_y] = jnp.where(halo_lanes, down, chunks[prev_y])


def one_section(ref, sigma, matrix, scale, x_low, x_high, y_low, y_high, reflect, emit):
    rows = rows_iota()
    lower = rows < 4
    m = matrix * scale

    def pair(first, second):
        return jnp.where(lower, jnp.float32(first), jnp.float32(second))

    to_low = [pair(m[0, 1], m[1, 0]), pair(m[0, 2], m[1, 3]), pair(m[0, 3], m[1, 2])]
    to_high = [pair(m[2, 0], m[3, 1]), pair(m[2, 1], m[3, 0]), pair(m[2, 3], m[3, 2])]
    lift = jnp.float32(lift_half * scale)
    six = [
        jnp.where((rows >= 2) & (rows < 4), lift, 0.0),
        jnp.where((rows >= 4) & (rows < 6), lift, 0.0),
    ]
    wall = [
        jnp.where(rows < 2, reflect * lift, 0.0),
        jnp.where(rows >= 6, reflect * lift, 0.0),
    ]
    z_face = [lower, rows >= 4]
    lanes = lanes_iota()
    even_row = (rows & 1) == 0

    def own(count, half, inner_only):
        face = (six[half] > 0.0) if inner_only else z_face[half]
        return jnp.where(face, -lift * (count + 1), -lift * count)

    diagonal = {
        (count, half, inner): own(count, half, inner)
        for count in range(3)
        for half in range(2)
        for inner in (False, True)
    }

    def weighted(field, fixed, index, axis):
        total = None
        for other in range(4):
            if other == index:
                continue
            a, b, half = fixed
            if axis == 0:
                a = other
            else:
                b = other
            term = jnp.float32(m[index, other]) * load(ref, field, a, b, half)
            total = term if total is None else total + term
        return total

    for a in range(4):
        for b in range(4):
            press = [load(ref, 0, a, b, h) for h in range(2)]
            vel = [[load(ref, 1 + i, a, b, h) for h in range(2)] for i in range(3)]

            def c_weighted(values, half):
                rolled = [sub_roll(v, 4) for v in values]
                if half == 0:
                    return (
                        to_low[0] * rolled[0] + to_low[1] * values[1] + to_low[2] * rolled[1]
                    )
                return (
                    to_high[0] * values[0] + to_high[1] * rolled[0] + to_high[2] * rolled[1]
                )

            sign = jnp.float32(sigma)
            e0 = press[0] - vel[2][0] if sigma > 0 else press[0] + vel[2][0]
            e1 = press[1] + vel[2][1] if sigma > 0 else press[1] - vel[2][1]
            z_terms = [
                six[0] * sub_roll(e1, -2) + wall[0] * e0,
                six[1] * sub_roll(e0, 2) + wall[1] * e1,
            ]
            count = (1 if a in (0, 3) else 0) + (1 if b in (0, 3) else 0)
            for half in range(2):
                fixed = (a, b, half)
                out_p = (
                    weighted(1, fixed, a, 0)
                    + weighted(2, fixed, b, 1)
                    + c_weighted(vel[2], half)
                )
                out_1 = weighted(0, fixed, a, 0)
                out_2 = weighted(0, fixed, b, 1)
                out_3 = c_weighted(press, half)
                out_p = out_p + diagonal[count, half, False] * press[half] + z_terms[half]
                out_1 = out_1 + diagonal[count, half, True] * vel[0][half]
                out_2 = out_2 + diagonal[count, half, True] * vel[1][half]
                out_3 = out_3 + diagonal[count, half, False] * vel[2][half]
                plus = (sigma > 0) == (half == 0)
                out_3 = out_3 + z_terms[half] if plus else out_3 - z_terms[half]
                turn = -2 if half == 0 else 2
                out_1 = out_1 + six[half] * sub_roll(vel[0][1 - half], turn)
                out_2 = out_2 + six[half] * sub_roll(vel[1][1 - half], turn)
                if a in (0, 3):
                    theirs = x_trace(ref, sigma, 3 - a, b, half)
                    if a == 0:
                        near = [
                            jnp.where(even_row, x_low(part, b, half), sub_roll(t, 1))
                            for part, t in enumerate(theirs)
                        ]
                    else:
                        near = [
                            jnp.where(even_row, sub_roll(t, -1), x_high(part, b, half))
                            for part, t in enumerate(theirs)
                        ]
                    near = [lift * n for n in near]
                    out_p = out_p + near[0]
                    plus = (sigma > 0) == (a == 0)
                    out_1 = out_1 + near[0] if plus else out_1 - near[0]
                    out_2 = out_2 + near[1]
                    out_3 = out_3 + near[2]
                if b in (0, 3):
                    theirs = y_trace(ref, sigma, a, 3 - b, half)
                    if b == 0:
                        near = [
                            jnp.where(lanes == 0, y_low(part, a, half), lane_roll(t, 1))
                            for part, t in enumerate(theirs)
                        ]
                    else:
                        near = [
                            jnp.where(lanes == 127, y_high(part, a, half), lane_roll(t, -1))
                            for part, t in enumerate(theirs)
                        ]
                    near = [lift * n for n in near]
                    out_p = out_p + near[0]
                    plus = (sigma > 0) == (b == 0)
                    out_2 = out_2 + near[0] if plus else out_2 - near[0]
                    out_1 = out_1 + near[1]
                    out_3 = out_3 + near[2]
                emit(a, b, half, [out_p, out_1, out_2, out_3])


def section_kernel(
    gx, gy, st, rg, ct, imp, wp, first, second, chunks, new_st, new_rg, grad, imp_grad, table
):
    me_x, me_y = lax.axis_index("gx"), lax.axis_index("gy")
    rows, lanes = rows_iota(), lanes_iota()
    even_me = (me_x & 1) == 0
    width = LANES // gx
    total = None
    blocks = []
    for group in range(gy // 2):
        block = jnp.zeros((8, LANES), jnp.float32)
        for x in range(gx):
            pair = chunks[x * gy + 2 * group] + chunks[x * gy + 2 * group + 1]
            total = pair if total is None else total + pair
            moved = lane_roll(pair, x * width - IMP_LANE)
            here = (lanes >= x * width) & (lanes < (x + 1) * width)
            block = jnp.where(here, moved, block)
        table[group * 8 : group * 8 + 8, :] = (block - 1.0) / (block + 1.0)
    patch_sum = jnp.where(
        lanes < SUM_LANE, pltpu.roll(total, SUM_LANE, 1), sub_roll(total, 4)
    )[:4]
    above = imp[...] + 1.0
    factor = time_step * section_b * lift_half * 2.0
    imp_grad[...] = patch_sum * jnp.float32(factor) / (above * above)
    patch = jnp.concatenate([wp[...], wp[...]], axis=0)
    low_of = patch & (LANES - 1)
    high_of = lax.shift_right_logical(patch, 7)
    reflect = jnp.zeros((8, LANES), jnp.float32)
    for high in range(4 * gy):
        line = jnp.broadcast_to(table[high : high + 1, :], (8, LANES))
        found = jnp.take_along_axis(line, low_of, axis=1)
        reflect = jnp.where(high_of == high, found, reflect)

    below = chunks[me_x * gy + lax.rem(me_y + gy - 1, gy)]
    ahead = chunks[me_x * gy + lax.rem(me_y + 1, gy)]

    def halos(number):
        def at(part, b):
            return pl.ds(((number * 3 + part) * 4 + b) * 8, 8)

        def x_low(part, b, half):
            got = jnp.where(even_me, second[at(part, b), :], first[at(part, b), :])
            return got if half == 0 else sub_roll(got, -1)

        def x_high(part, b, half):
            got = jnp.where(even_me, first[at(part, b), :], second[at(part, b), :])
            return got if half == 0 else sub_roll(got, 1)

        def lane(part, a, half):
            return (number * 3 + part) * 8 + a * 2 + half

        def y_low(part, a, half):
            return lane_roll(below, -lane(part, a, half))

        def y_high(part, a, half):
            return lane_roll(ahead, 127 - lane(part, a, half))

        return x_low, x_high, y_low, y_high

    matrix = derivative_table()
    matrix = matrix * (1.0 - np.eye(4))

    def emit_state(a, b, half, outs):
        for field in range(4):
            at = pl.ds(row_of(field, a, b, half), 8)
            following = jnp.float32(section_a) * rg[at, :] + outs[field]
            new_rg[at, :] = following
            new_st[at, :] = st[at, :] + jnp.float32(section_b) * following

    def emit_grad(a, b, half, outs):
        for field in range(4):
            at = pl.ds(row_of(field, a, b, half), 8)
            grad[at, :] = ct[at, :] + outs[field]

    one_section(st, 1, -matrix, time_step, *halos(0), reflect, emit_state)
    one_section(ct, -1, -matrix.T, time_step * section_b, *halos(1), reflect, emit_grad)


def per_device(state, register, cotangent, impedance, wall_patch):
    gx, gy = lax.axis_size("gx"), lax.axis_size("gy")
    flat = (1024, LANES)
    st, rg, ct = (v.reshape(flat) for v in (state, register, cotangent))
    imp = impedance.reshape(4, LANES)
    wp = wall_patch.reshape(4, LANES)
    f32 = jnp.float32
    first, second, chunks = pl.pallas_call(
        functools.partial(pack_kernel, gx, gy),
        out_shape=(
            jax.ShapeDtypeStruct((192, LANES), f32),
            jax.ShapeDtypeStruct((192, LANES), f32),
            jax.ShapeDtypeStruct((gx * gy, 8, LANES), f32),
        ),
        name="pack",
    )(st, ct, imp, wp)
    near = [(i, i ^ 1) for i in range(gx)]
    far = [(i, (i + 1) % gx if i % 2 else (i - 1) % gx) for i in range(gx)]
    first = lax.ppermute(first, "gx", near)
    second = lax.ppermute(second, "gx", far)
    chunks = lax.all_to_all(chunks, ("gx", "gy"), 0, 0)
    new_st, new_rg, grad, imp_grad = pl.pallas_call(
        functools.partial(section_kernel, gx, gy),
        out_shape=(
            jax.ShapeDtypeStruct(flat, f32),
            jax.ShapeDtypeStruct(flat, f32),
            jax.ShapeDtypeStruct(flat, f32),
            jax.ShapeDtypeStruct((4, LANES), f32),
        ),
        scratch_shapes=[pltpu.VMEM((4 * gy, LANES), f32)],
        compiler_params=pltpu.CompilerParams(vmem_limit_bytes=24 * 2**20),
        name="section",
    )(st, rg, ct, imp, wp, first, second, chunks)
    return (
        new_st.reshape(state.shape),
        new_rg.reshape(state.shape),
        grad.reshape(state.shape),
        imp_grad.reshape(impedance.shape),
    )


def solution(mesh):
    fields = P(None, None, None, "gx", "gy")
    return jax.shard_map(
        per_device,
        mesh=mesh,
        in_specs=(fields, fields, fields, P("gy"), P(None, "gx", "gy")),
        out_specs=(fields, fields, fields, P("gy")),
        check_vma=False,
    )
```

profile of v0, /device:TPU:0, one launch (start us, length us, event | category | flops | bytes accessed | tf_op | source)
XLA Modules:
  0.0 21.4 jit_solution(5712739054825865164)
XLA Ops:
  0.6 0.0 copy-start
  0.6 0.0 copy-start.1
  0.7 2.2 %pack.1 = (f32[192,128]{1,0:T(8,128)}, f32[192,128]{1,0:T(8,128)}, f32[32,8,128]{2,1,0:T(8,128)}) custom-call(f32[1024,128]{1,0:T(8,128)} %bitcast.9, f32[1024,128]{1,0:T(8,128)} %bitcast.11, f32[4,128]{1,0:T(4,128)} %bitcast.14, s32[4,128]{1,0:T(4,128)} %bitcast.16), custom_call_target="tpu_custom_call" | custom-call | tf_op jit(solution)/shard_map/pack/pallas_call | solution.py:368
  2.9 0.0 copy-start.6
  2.9 0.0 copy-start.5
  2.9 7.3 %all-to-all-start = ((f32[32,8,128]{2,1,0:T(8,128)}), f32[32,8,128]{2,1,0:T(8,128)S(1)}, u32[]{:S(2)}, u32[]{:S(2)}) async-start(f32[32,8,128]{2,1,0:T(8,128)} %get-tuple-element.13), calls=%async_computation | async-start | bytes 262144 | tf_op jit(solution)/shard_map/all_to_all | solution.py:381
  10.2 0.0 copy-start.4
  10.2 0.0 copy-done.6
  10.2 0.0 copy-start.3
  10.2 0.3 %collective-permute-start = (f32[192,128]{1,0:T(8,128)S(1)}, f32[192,128]{1,0:T(8,128)S(1)}, u32[]{:S(2)}, u32[]{:S(2)}) collective-permute-start(f32[192,128]{1,0:T(8,128)S(1)} %copy-done.6), channel_id=1, source_target_pairs={{0,4},{4,0},{8,12},{12,8},{16,20},{20,16},{24,28},{28,24},{1,5},{5... | collective-permute-start | bytes 294920 | tf_op jit(solution)/shard_map/ppermute | solution.py:379
  10.5 0.0 copy-done.5
  10.5 2.5 %collective-permute-start.1 = (f32[192,128]{1,0:T(8,128)S(1)}, f32[192,128]{1,0:T(8,128)S(1)}, u32[]{:S(2)}, u32[]{:S(2)}) collective-permute-start(f32[192,128]{1,0:T(8,128)S(1)} %copy-done.5), channel_id=1, source_target_pairs={{0,28},{4,8},{8,4},{12,16},{16,12},{20,24},{24,20},{28,0},{1,29},{... | collective-permute-start | bytes 294920 | tf_op jit(solution)/shard_map/ppermute | solution.py:380
  13.1 0.0 collective-permute-done.first
  13.1 3.9 %collective-permute-done.1.second = f32[192,128]{1,0:T(8,128)S(1)} collective-permute-done((f32[192,128]{1,0:T(8,128)S(1)}, f32[192,128]{1,0:T(8,128)S(1)}, u32[]{:S(2)}, u32[]{:S(2)}) %collective-permute-start.1) | collective-permute-done | bytes 98336 | tf_op jit(solution)/shard_map/ppermute | solution.py:380
  16.9 1.7 %all-to-all-done.chunks = f32[32,8,128]{2,1,0:T(8,128)S(1)} async-done(((f32[32,8,128]{2,1,0:T(8,128)}), f32[32,8,128]{2,1,0:T(8,128)S(1)}, u32[]{:S(2)}, u32[]{:S(2)}) %all-to-all-start) | async-done | bytes 131104 | tf_op jit(solution)/shard_map/all_to_all | solution.py:381
  18.6 0.0 copy-done
  18.6 0.0 copy-done.1
  18.6 0.0 copy-done.4
  18.6 0.0 copy-done.3
  18.6 0.0 copy-start.2
  18.6 1.0 %copy-done.2 = f32[4,64,2,2,128]{4,3,2,1,0:T(2,128)S(1)} copy-done((f32[4,64,2,2,128]{4,3,2,1,0:T(2,128)S(1)}, f32[4,64,2,2,128]{4,3,2,1,0:T(2,128)}, u32[]{:S(2)}) %copy-start.2) | copy-done | bytes 524312
  19.7 1.7 %section.1 = (f32[1024,128]{1,0:T(8,128)}, f32[1024,128]{1,0:T(8,128)}, f32[1024,128]{1,0:T(8,128)}, f32[4,128]{1,0:T(4,128)}) custom-call(f32[1024,128]{1,0:T(8,128)S(1)} %bitcast.10, f32[1024,128]{1,0:T(8,128)S(1)} %bitcast.13, f32[1024,128]{1,0:T(8,128)S(1)} %bitcast.12, f32[4,128]{1,0:T(4,128)S(1)} %bitcast.15, s32[4,128]{1,0:T(4,128)S(1)} %bitcast.17, ...), custom_call_target="tpu_custom_call" | custom-call | tf_op jit(solution)/shard_map/section/pallas_call | solution.py:382
Async XLA Ops:
  0.6 18.0 %copy-start = (f32[4,64,2,2,128]{4,3,2,1,0:T(2,128)S(1)}, f32[4,64,2,2,128]{4,3,2,1,0:T(2,128)}, u32[]{:S(2)}) copy-start(f32[4,64,2,2,128]{4,3,2,1,0:T(2,128)} %param.5) | copy-start | bytes 1572868
  0.6 18.0 %copy-start.1 = (f32[4,64,2,2,128]{4,3,2,1,0:T(2,128)S(1)}, f32[4,64,2,2,128]{4,3,2,1,0:T(2,128)}, u32[]{:S(2)}) copy-start(f32[4,64,2,2,128]{4,3,2,1,0:T(2,128)} %param.7) | copy-start | bytes 1572868
  2.9 7.3 %copy-start.6 = (f32[192,128]{1,0:T(8,128)S(1)}, f32[192,128]{1,0:T(8,128)}, u32[]{:S(2)}) copy-start(f32[192,128]{1,0:T(8,128)} %get-tuple-element.11) | copy-start | bytes 294916
  2.9 7.7 %copy-start.5 = (f32[192,128]{1,0:T(8,128)S(1)}, f32[192,128]{1,0:T(8,128)}, u32[]{:S(2)}) copy-start(f32[192,128]{1,0:T(8,128)} %get-tuple-element.12) | copy-start | bytes 294916
  2.9 15.7 %all-to-all-start = ((f32[32,8,128]{2,1,0:T(8,128)}), f32[32,8,128]{2,1,0:T(8,128)S(1)}, u32[]{:S(2)}, u32[]{:S(2)}) async-start(f32[32,8,128]{2,1,0:T(8,128)} %get-tuple-element.13), calls=%async_computation | async-start | bytes 262144 | tf_op jit(solution)/shard_map/all_to_all | solution.py:381
  10.2 8.4 %copy-start.4 = (s32[2,2,128]{2,1,0:T(2,128)S(1)}, s32[2,2,128]{2,1,0:T(2,128)}, u32[]{:S(2)}) copy-start(s32[2,2,128]{2,1,0:T(2,128)} %param.9) | copy-start | bytes 6148
  10.2 8.4 %copy-start.3 = (f32[512]{0:T(512)S(1)}, f32[512]{0:T(512)}, u32[]{:S(2)}) copy-start(f32[512]{0:T(512)} %param.8) | copy-start | bytes 6148
  10.2 2.9 %collective-permute-start = (f32[192,128]{1,0:T(8,128)S(1)}, f32[192,128]{1,0:T(8,128)S(1)}, u32[]{:S(2)}, u32[]{:S(2)}) collective-permute-start(f32[192,128]{1,0:T(8,128)S(1)} %copy-done.6), channel_id=1, source_target_pairs={{0,4},{4,0},{8,12},{12,8},{16,20},{20,16},{24,28},{28,24},{1,5},{5... | collective-permute-start | bytes 294920 | tf_op jit(solution)/shard_map/ppermute | solution.py:379
  10.5 6.4 %collective-permute-start.1 = (f32[192,128]{1,0:T(8,128)S(1)}, f32[192,128]{1,0:T(8,128)S(1)}, u32[]{:S(2)}, u32[]{:S(2)}) collective-permute-start(f32[192,128]{1,0:T(8,128)S(1)} %copy-done.5), channel_id=1, source_target_pairs={{0,28},{4,8},{8,4},{12,16},{16,12},{20,24},{24,20},{28,0},{1,29},{... | collective-permute-start | bytes 294920 | tf_op jit(solution)/shard_map/ppermute | solution.py:380
  18.6 1.0 %copy-start.2 = (f32[4,64,2,2,128]{4,3,2,1,0:T(2,128)S(1)}, f32[4,64,2,2,128]{4,3,2,1,0:T(2,128)}, u32[]{:S(2)}) copy-start(f32[4,64,2,2,128]{4,3,2,1,0:T(2,128)} %param.6) | copy-start | bytes 1572868
where the time goes:
time: 21.6 us; the launch traced here: 21.4 us
  starting transfers between devices  10.1 us (47%)
  waiting for transfers between devices  5.52 us (26%)
  Pallas kernels  3.95 us (18%)
  local copies, waits for them, and re-layouts  1.07 us (5%)
  between operations  0.7 us (3%)
    all_to_all x1, starting transfers between devices, per_device(): chunks = lax.all_to_all(chunks, ('gx', 'gy'), 0, 0)  7.3 us
    ppermute x1, waiting for transfers between devices, per_device(): second = lax.ppermute(second, 'gx', far)  3.86 us
    ppermute x1, starting transfers between devices, per_device(): second = lax.ppermute(second, 'gx', far)  2.53 us
    pallas_call x1, Pallas kernels, per_device(): pl.pallas_call(functools.partial(pack_kernel, gx, gy), out_shape=(jax.Sha...  2.22 us
    pallas_call x1, Pallas kernels, per_device(): pl.pallas_call(functools.partial(section_kernel, gx, gy), out_shape=(jax....  1.72 us
    all_to_all x1, waiting for transfers between devices, per_device(): chunks = lax.all_to_all(chunks, ('gx', 'gy'), 0, 0)  1.65 us
    unnamed x14, local copies, waits for them, and re-layouts  1.07 us
  transfers between devices with their start and end apart: 3, of which 2 were waited for; matrix products, arithmetic and copies ran while one was open for 0% of the time, Pallas kernels for 0%

commit v1 on v0

v1 whole, which is shorter than its diff:
```python
import functools
import math

import jax
import jax.numpy as jnp
import numpy as np
from jax import lax
from jax.experimental import pallas as pl
from jax.experimental.pallas import tpu as pltpu
from jax.sharding import PartitionSpec as P

time_step = 0.02
section_a = -0.4178904745
section_b = 0.3792103129
lift_half = 6.0

LANES = 128
HALO_LANES = 48
IMP_LANE = 48
SUM_LANE = 64


def derivative_table():
    points = np.array([-1.0, -1.0 / math.sqrt(5.0), 1.0 / math.sqrt(5.0), 1.0])
    identity = np.eye(4)
    distance = points[:, None] - points[None, :] + identity
    barycentric = 1.0 / np.prod(distance, axis=1)
    matrix = barycentric[None, :] / (barycentric[:, None] * distance)
    matrix = matrix * (1.0 - identity)
    matrix = matrix - identity * matrix.sum(axis=1)[:, None]
    return 2.0 * matrix


def rows_at(b, half):
    return pl.ds(b * 16 + half * 8, 8)


def load(ref, field, a, b, half):
    return ref[field, a, rows_at(b, half), :]


INTERIOR_FLOPS = 30000000000


def sub_roll(value, shift):
    return pltpu.roll(value, shift % 8, 0)


def lane_roll(value, shift):
    shift = shift % LANES
    return value if shift == 0 else pltpu.roll(value, shift, 1)


def rows_iota():
    return lax.broadcasted_iota(jnp.int32, (8, LANES), 0)


def lanes_iota():
    return lax.broadcasted_iota(jnp.int32, (8, LANES), 1)


def x_trace(ref, sigma, a, b, half):
    flip = sigma if a == 3 else -sigma
    press, normal = load(ref, 0, a, b, half), load(ref, 1, a, b, half)
    mixed = press + normal if flip > 0 else press - normal
    return [mixed, load(ref, 2, a, b, half), load(ref, 3, a, b, half)]


def y_trace(ref, sigma, a, b, half):
    flip = sigma if b == 3 else -sigma
    press, normal = load(ref, 0, a, b, half), load(ref, 2, a, b, half)
    mixed = press + normal if flip > 0 else press - normal
    return [mixed, load(ref, 1, a, b, half), load(ref, 3, a, b, half)]


def pack_kernel(
    gx, gy, st_in, ct_in, imp_in, wp_in, st, ct, imp, wp, first, second, chunks, sems, small, one_hot
):
    me_x, me_y = lax.axis_index("gx"), lax.axis_index("gy")
    rows, lanes = rows_iota(), lanes_iota()
    even_row = (rows & 1) == 0
    even_me = (me_x & 1) == 0
    loads = {}
    for number, (source, target) in enumerate(((imp_in, imp), (wp_in, wp))):
        loads[number, 4] = pltpu.make_async_copy(source, target, small.at[number])
    loads[1, 4].start()
    for a in (0, 3, 1, 2):
        for number, (source, target) in enumerate(((st_in, st), (ct_in, ct))):
            loads[number, a] = pltpu.make_async_copy(
                source.at[:, a], target.at[:, a], sems.at[number, a]
            )
            loads[number, a].start()
    loads[0, 4].start()
    up = jnp.zeros((8, LANES), jnp.float32)
    down = jnp.zeros((8, LANES), jnp.float32)
    floor = jnp.zeros((8, LANES), jnp.float32)
    ceil = jnp.zeros((8, LANES), jnp.float32)

    def columns_and_walls(a, up, down, floor, ceil):
        for number, (ref, sigma) in enumerate(((st, 1), (ct, -1))):
            for half in range(2):
                high = y_trace(ref, sigma, a, 3, half)
                low = y_trace(ref, sigma, a, 0, half)
                for part in range(3):
                    k = (number * 3 + part) * 8 + a * 2 + half
                    up = jnp.where(lanes == k, lane_roll(high[part], k - 127), up)
                    down = jnp.where(lanes == k, lane_roll(low[part], k), down)
        for b in range(4):
            floor += (load(st, 0, a, b, 0) - load(st, 3, a, b, 0)) * (
                load(ct, 0, a, b, 0) + load(ct, 3, a, b, 0)
            )
            ceil += (load(st, 0, a, b, 1) + load(st, 3, a, b, 1)) * (
                load(ct, 0, a, b, 1) - load(ct, 3, a, b, 1)
            )
        return up, down, floor, ceil

    loads[1, 4].wait()
    groups = 4 * gy
    count = 4 * LANES
    patch = jnp.concatenate([wp[r : r + 1, :] for r in range(4)], axis=1)
    high_of = lax.shift_right_logical(patch, 7)
    low_of = patch & (LANES - 1)
    hot = lax.broadcasted_iota(jnp.int32, (LANES, count), 0) == low_of
    one_hot[...] = jnp.where(hot, 1.0, 0.0).astype(jnp.bfloat16)
    loads[0, 0].wait()
    loads[1, 0].wait()
    up, down, floor, ceil = columns_and_walls(0, up, down, floor, ceil)
    loads[0, 3].wait()
    loads[1, 3].wait()
    up, down, floor, ceil = columns_and_walls(3, up, down, floor, ceil)
    for number, (ref, sigma) in enumerate(((st, 1), (ct, -1))):
        for b in range(4):
            high = [x_trace(ref, sigma, 3, b, half) for half in range(2)]
            low = [x_trace(ref, sigma, 0, b, half) for half in range(2)]
            for part in range(3):
                to_right = jnp.where(even_row, sub_roll(high[0][part], -1), high[1][part])
                to_left = jnp.where(even_row, low[1][part], sub_roll(low[0][part], 1))
                at = pl.ds(((number * 3 + part) * 4 + b) * 8, 8)
                first[at, :] = jnp.where(even_me, to_right, to_left)
                second[at, :] = jnp.where(even_me, to_left, to_right)
    for a in (1, 2):
        loads[0, a].wait()
        loads[1, a].wait()
        up, down, floor, ceil = columns_and_walls(a, up, down, floor, ceil)
    loads[0, 4].wait()
    values = jnp.concatenate([floor[0:1], floor[1:2], ceil[6:7], ceil[7:8]], axis=1)
    chosen = lax.broadcasted_iota(jnp.int32, (groups, count), 0) == high_of
    spread = jnp.where(chosen, jnp.broadcast_to(values, (groups, count)), 0.0)
    top = spread.astype(jnp.bfloat16)
    rest = spread - top.astype(jnp.float32)
    middle = rest.astype(jnp.bfloat16)
    last = (rest - middle.astype(jnp.float32)).astype(jnp.bfloat16)
    pieces = jnp.concatenate([top, middle, last], axis=0)
    sums = lax.dot_general(
        pieces, one_hot[...], (((1,), (1,)), ((), ())), preferred_element_type=jnp.float32
    )
    sums = sums[:groups] + sums[groups : 2 * groups] + sums[2 * groups :]
    width = LANES // gx
    shard = jnp.concatenate([imp[...], imp[...]], axis=0)
    placed = pltpu.roll(shard, (IMP_LANE - me_x * width + LANES) % LANES, 1)
    odd_me_y = me_y & 1
    imp_here = (
        (lanes >= IMP_LANE)
        & (lanes < IMP_LANE + width)
        & (lax.shift_right_logical(rows, 2) == odd_me_y)
    )
    common = jnp.where(imp_here, placed, 0.0)
    upper_lanes = lanes >= SUM_LANE
    tiles = []
    for target in range(gy):
        part = sums[target * 4 : target * 4 + 4]
        both = jnp.concatenate([pltpu.roll(part, SUM_LANE, 1), part], axis=0)
        tiles.append(jnp.where(upper_lanes, both, common))
    for x in range(gx):
        for target in range(gy):
            chunks[x * gy + target] = tiles[target]
    halo_lanes = lanes < HALO_LANES
    next_y = me_x * gy + lax.rem(me_y + 1, gy)
    prev_y = me_x * gy + lax.rem(me_y + gy - 1, gy)
    chunks[next_y] = jnp.where(halo_lanes, up, chunks[next_y])
    chunks[prev_y] = jnp.where(halo_lanes, down, chunks[prev_y])


def interior(ref, sigma, matrix, scale, x_low, x_high, emit):
    rows = rows_iota()
    lower = rows < 4
    m = matrix * scale

    def pair(first, second):
        return jnp.where(lower, jnp.float32(first), jnp.float32(second))

    to_low = [pair(m[0, 1], m[1, 0]), pair(m[0, 2], m[1, 3]), pair(m[0, 3], m[1, 2])]
    to_high = [pair(m[2, 0], m[3, 1]), pair(m[2, 1], m[3, 0]), pair(m[2, 3], m[3, 2])]
    lift = jnp.float32(lift_half * scale)
    six = [
        jnp.where((rows >= 2) & (rows < 4), lift, 0.0),
        jnp.where((rows >= 4) & (rows < 6), lift, 0.0),
    ]
    z_face = [lower, rows >= 4]
    lanes = lanes_iota()
    even_row = (rows & 1) == 0

    def own(count, half, inner_only):
        face = (six[half] > 0.0) if inner_only else z_face[half]
        return jnp.where(face, -lift * (count + 1), -lift * count)

    diagonal = {
        (count, half, inner): own(count, half, inner)
        for count in range(3)
        for half in range(2)
        for inner in (False, True)
    }

    def weighted(field, fixed, index, axis):
        total = None
        for other in range(4):
            if other == index:
                continue
            a, b, half = fixed
            if axis == 0:
                a = other
            else:
                b = other
            term = jnp.float32(m[index, other]) * load(ref, field, a, b, half)
            total = term if total is None else total + term
        return total

    def c_weighted(values, rolled, half):
        if half == 0:
            return to_low[0] * rolled[0] + to_low[1] * values[1] + to_low[2] * rolled[1]
        return to_high[0] * values[0] + to_high[1] * rolled[0] + to_high[2] * rolled[1]

    for a in range(4):
        for b in range(4):
            press = [load(ref, 0, a, b, h) for h in range(2)]
            vel = [[load(ref, 1 + i, a, b, h) for h in range(2)] for i in range(3)]
            press_rolled = [sub_roll(v, 4) for v in press]
            up_rolled = [sub_roll(v, 4) for v in vel[2]]
            e0, e1 = wall_traces(press, vel[2], sigma)
            z_terms = [six[0] * sub_roll(e1, -2), six[1] * sub_roll(e0, 2)]
            count = (1 if a in (0, 3) else 0) + (1 if b in (0, 3) else 0)
            for half in range(2):
                fixed = (a, b, half)
                out_p = (
                    weighted(1, fixed, a, 0)
                    + weighted(2, fixed, b, 1)
                    + c_weighted(vel[2], up_rolled, half)
                )
                out_1 = weighted(0, fixed, a, 0)
                out_2 = weighted(0, fixed, b, 1)
                out_3 = c_weighted(press, press_rolled, half)
                out_p = out_p + diagonal[count, half, False] * press[half] + z_terms[half]
                out_1 = out_1 + diagonal[count, half, True] * vel[0][half]
                out_2 = out_2 + diagonal[count, half, True] * vel[1][half]
                out_3 = out_3 + diagonal[count, half, False] * vel[2][half]
                plus = (sigma > 0) == (half == 0)
                out_3 = out_3 + z_terms[half] if plus else out_3 - z_terms[half]
                turn = -2 if half == 0 else 2
                out_1 = out_1 + six[half] * sub_roll(vel[0][1 - half], turn)
                out_2 = out_2 + six[half] * sub_roll(vel[1][1 - half], turn)
                if a in (0, 3):
                    theirs = x_trace(ref, sigma, 3 - a, b, half)
                    if a == 0:
                        near = [
                            jnp.where(even_row, x_low(part, b, half), sub_roll(t, 1))
                            for part, t in enumerate(theirs)
                        ]
                    else:
                        near = [
                            jnp.where(even_row, sub_roll(t, -1), x_high(part, b, half))
                            for part, t in enumerate(theirs)
                        ]
                    near = [lift * n for n in near]
                    out_p = out_p + near[0]
                    plus = (sigma > 0) == (a == 0)
                    out_1 = out_1 + near[0] if plus else out_1 - near[0]
                    out_2 = out_2 + near[1]
                    out_3 = out_3 + near[2]
                if b in (0, 3):
                    theirs = y_trace(ref, sigma, a, 3 - b, half)
                    if b == 0:
                        weight = jnp.where(lanes == 0, 0.0, lift)
                        near = [weight * lane_roll(t, 1) for t in theirs]
                    else:
                        weight = jnp.where(lanes == 127, 0.0, lift)
                        near = [weight * lane_roll(t, -1) for t in theirs]
                    out_p = out_p + near[0]
                    plus = (sigma > 0) == (b == 0)
                    out_2 = out_2 + near[0] if plus else out_2 - near[0]
                    out_1 = out_1 + near[1]
                    out_3 = out_3 + near[2]
                emit(a, b, half, (out_p, out_1, out_2, out_3))


def wall_traces(press, vertical, sigma):
    if sigma > 0:
        return press[0] - vertical[0], press[1] + vertical[1]
    return press[0] + vertical[0], press[1] - vertical[1]


def interior_kernel(
    st, ct, first, second, rg_in, new_st, new_rg, grad, st_out, rg_out, grad_out, rg, sems
):
    me_x = lax.axis_index("gx")
    load_rg = pltpu.make_async_copy(rg_in, rg, sems.at[3])
    load_rg.start()
    even_me = (me_x & 1) == 0

    def halos(number):
        def at(part, b):
            return pl.ds(((number * 3 + part) * 4 + b) * 8, 8)

        def x_low(part, b, half):
            got = jnp.where(even_me, second[at(part, b), :], first[at(part, b), :])
            return got if half == 0 else sub_roll(got, -1)

        def x_high(part, b, half):
            got = jnp.where(even_me, first[at(part, b), :], second[at(part, b), :])
            return got if half == 0 else sub_roll(got, 1)

        return x_low, x_high

    matrix = derivative_table()
    matrix = matrix * (1.0 - np.eye(4))

    def store(source, target, kind):
        inner = (pl.ds(1, 2), slice(None), pl.ds(16, 32))
        copy = pltpu.make_async_copy(source.at[inner], target.at[inner], sems.at[kind])
        copy.start()
        return copy

    def emit_grad(a, b, half, outs):
        at = rows_at(b, half)
        for field in range(4):
            grad[field, a, at, :] = ct[field, a, at, :] + outs[field]

    def emit_state(a, b, half, outs):
        at = rows_at(b, half)
        for field in range(4):
            following = jnp.float32(section_a) * rg[field, a, at, :] + outs[field]
            new_rg[field, a, at, :] = following
            new_st[field, a, at, :] = st[field, a, at, :] + jnp.float32(section_b) * following

    interior(ct, -1, -matrix.T, time_step * section_b, *halos(1), emit_grad)
    stores = [store(grad, grad_out, 2)]
    load_rg.wait()
    interior(st, 1, -matrix, time_step, *halos(0), emit_state)
    stores += [store(new_st, st_out, 0), store(new_rg, rg_out, 1)]
    for copy in stores:
        copy.wait()


def finish_kernel(
    gx,
    gy,
    st,
    ct,
    imp,
    wp,
    new_st,
    new_rg,
    grad,
    chunks,
    st_prior,
    rg_prior,
    grad_prior,
    st_out,
    rg_out,
    grad_out,
    imp_out,
    table,
    imp_grad,
    full_st,
    full_rg,
    full_grad,
    sems,
    last_sem,
):
    del st_prior, rg_prior, grad_prior
    me_x, me_y = lax.axis_index("gx"), lax.axis_index("gy")
    rows, lanes = rows_iota(), lanes_iota()
    stores = []

    def store(source, target, at, kind, piece):
        copy = pltpu.make_async_copy(source.at[at], target.at[at], sems.at[kind, piece])
        copy.start()
        stores.append(copy)

    def store_lines(source, target, b, kind):
        every = slice(None)
        if b in (0, 3):
            store(source, target, (every, every, pl.ds(b * 16, 16)), kind, b)
        if b == 2:
            for piece, field in ((1, 0), (2, 3)):
                at = (pl.ds(field, 1), every, pl.ds(16, 32))
                store(source, target, at, kind, piece)

    width = LANES // gx
    total = None
    for group in range(gy // 2):
        block = jnp.zeros((8, LANES), jnp.float32)
        for x in range(gx):
            pair = chunks[x * gy + 2 * group] + chunks[x * gy + 2 * group + 1]
            total = pair if total is None else total + pair
            moved = lane_roll(pair, x * width - IMP_LANE)
            here = (lanes >= x * width) & (lanes < (x + 1) * width)
            block = jnp.where(here, moved, block)
        table[group * 8 : group * 8 + 8, :] = (block - 1.0) / (block + 1.0)
    patch_sum = jnp.where(
        lanes < SUM_LANE, pltpu.roll(total, SUM_LANE, 1), sub_roll(total, 4)
    )[:4]
    above = imp[...] + 1.0
    factor = time_step * section_b * lift_half * 2.0
    imp_grad[...] = patch_sum * jnp.float32(factor) / (above * above)
    send_sum = pltpu.make_async_copy(imp_grad, imp_out, last_sem.at[0])
    send_sum.start()
    patch = jnp.concatenate([wp[...], wp[...]], axis=0)
    low_of = patch & (LANES - 1)
    high_of = lax.shift_right_logical(patch, 7)
    reflect = jnp.zeros((8, LANES), jnp.float32)
    for high in range(4 * gy):
        line = jnp.broadcast_to(table[high : high + 1, :], (8, LANES))
        found = jnp.take_along_axis(line, low_of, axis=1)
        reflect = jnp.where(high_of == high, found, reflect)

    below = chunks[me_x * gy + lax.rem(me_y + gy - 1, gy)]
    ahead = chunks[me_x * gy + lax.rem(me_y + 1, gy)]

    for number, ref, sigma, scale in (
        (1, ct, -1, time_step * section_b),
        (0, st, 1, time_step),
    ):
        lift = jnp.float32(lift_half * scale)
        wall = [
            jnp.where(rows < 2, reflect * lift, 0.0),
            jnp.where(rows >= 6, reflect * lift, 0.0),
        ]
        first_lane = jnp.where(lanes == 0, lift, 0.0)
        last_lane = jnp.where(lanes == LANES - 1, lift, 0.0)
        for b in (0, 3, 1, 2):
            for a in range(4):
                press = [load(ref, 0, a, b, h) for h in range(2)]
                vertical = [load(ref, 3, a, b, h) for h in range(2)]
                traces = wall_traces(press, vertical, sigma)
                for half in range(2):
                    term = wall[half] * traces[half]
                    plus = (sigma > 0) == (half == 0)
                    outs = {0: term, 3: term if plus else -term}
                    if b in (0, 3):
                        near = []
                        for part in range(3):
                            k = (number * 3 + part) * 8 + a * 2 + half
                            if b == 0:
                                near.append(first_lane * lane_roll(below, -k))
                            else:
                                near.append(last_lane * lane_roll(ahead, LANES - 1 - k))
                        outs[0] = outs[0] + near[0]
                        plus = (sigma > 0) == (b == 0)
                        outs[2] = near[0] if plus else -near[0]
                        outs[1] = near[1]
                        outs[3] = outs[3] + near[2]
                    at = rows_at(b, half)
                    for field, more in outs.items():
                        if number == 0:
                            full_rg[field, a, at, :] = new_rg[field, a, at, :] + more
                            full_st[field, a, at, :] = (
                                new_st[field, a, at, :] + jnp.float32(section_b) * more
                            )
                        else:
                            full_grad[field, a, at, :] = grad[field, a, at, :] + more
            if number == 0:
                store_lines(full_rg, rg_out, b, 1)
                store_lines(full_st, st_out, b, 0)
            else:
                store_lines(full_grad, grad_out, b, 2)
    for copy in stores:
        copy.wait()
    send_sum.wait()


def per_device(state, register, cotangent, impedance, wall_patch):
    gx, gy = lax.axis_size("gx"), lax.axis_size("gy")
    flat = (4, 4, 64, LANES)
    st, rg, ct = (v.reshape(flat) for v in (state, register, cotangent))
    imp = impedance.reshape(4, LANES)
    wp = wall_patch.reshape(4, LANES)
    f32 = jnp.float32
    any_place = pl.BlockSpec(memory_space=pltpu.HBM)
    on_chip = pl.BlockSpec(memory_space=pltpu.VMEM)
    whole = pltpu.VMEM(flat, f32)
    params = pltpu.CompilerParams(vmem_limit_bytes=8 * 2**20)
    halo = pltpu.VMEM((192, LANES), f32)
    st, ct, imp, wp, first, second, chunks = pl.pallas_call(
        functools.partial(pack_kernel, gx, gy),
        in_specs=[any_place] * 4,
        out_specs=[on_chip] * 7,
        out_shape=(
            whole,
            whole,
            pltpu.VMEM((4, LANES), f32),
            pltpu.VMEM((4, LANES), jnp.int32),
            halo,
            halo,
            pltpu.VMEM((gx * gy, 8, LANES), f32),
        ),
        scratch_shapes=[
            pltpu.SemaphoreType.DMA((2, 4)),
            pltpu.SemaphoreType.DMA((2,)),
            pltpu.VMEM((LANES, 4 * LANES), jnp.bfloat16),
        ],
        compiler_params=params,
        name="pack",
    )(*(pltpu.with_memory_space_constraint(v, pltpu.HBM) for v in (st, ct, imp, wp)))
    near = [(i, i ^ 1) for i in range(gx)]
    far = [(i, (i + 1) % gx if i % 2 else (i - 1) % gx) for i in range(gx)]
    first = lax.ppermute(first, "gx", near)
    second = lax.ppermute(second, "gx", far)
    chunks = lax.all_to_all(chunks, ("gx", "gy"), 0, 0)
    result = pltpu.HBM(flat, f32)
    new_st, new_rg, grad, st_out, rg_out, grad_out = pl.pallas_call(
        interior_kernel,
        in_specs=[on_chip] * 4 + [any_place],
        out_specs=[on_chip] * 3 + [any_place] * 3,
        out_shape=(whole, whole, whole, result, result, result),
        scratch_shapes=[pltpu.VMEM(flat, f32), pltpu.SemaphoreType.DMA((4,))],
        compiler_params=params,
        cost_estimate=pl.CostEstimate(
            flops=INTERIOR_FLOPS, bytes_accessed=2400000, transcendentals=0
        ),
        name="interior",
    )(st, ct, first, second, pltpu.with_memory_space_constraint(rg, pltpu.HBM))
    new_st, new_rg, grad, imp_grad = pl.pallas_call(
        functools.partial(finish_kernel, gx, gy),
        in_specs=[on_chip] * 8 + [any_place] * 3,
        out_specs=[any_place] * 4,
        out_shape=(result, result, result, pltpu.HBM((4, LANES), f32)),
        input_output_aliases={8: 0, 9: 1, 10: 2},
        scratch_shapes=[
            pltpu.VMEM((4 * gy, LANES), f32),
            pltpu.VMEM((4, LANES), f32),
            pltpu.VMEM(flat, f32),
            pltpu.VMEM(flat, f32),
            pltpu.VMEM(flat, f32),
            pltpu.SemaphoreType.DMA((3, 4)),
            pltpu.SemaphoreType.DMA((1,)),
        ],
        compiler_params=params,
        name="finish",
    )(st, ct, imp, wp, new_st, new_rg, grad, chunks, st_out, rg_out, grad_out)
    return (
        new_st.reshape(state.shape),
        new_rg.reshape(state.shape),
        grad.reshape(state.shape),
        imp_grad.reshape(impedance.shape),
    )


def solution(mesh):
    fields = P(None, None, None, "gx", "gy")
    return jax.shard_map(
        per_device,
        mesh=mesh,
        in_specs=(fields, fields, fields, P("gy"), P(None, "gx", "gy")),
        out_specs=(fields, fields, fields, P("gy")),
        check_vma=False,
    )
```

time: 21.6 us -> 21.1 us (0.977)
  starting transfers between devices: 10.1 us -> 8.05 us
  Pallas kernels: 3.95 us -> 5.91 us
  local copies, waits for them, and re-layouts: 1.07 us -> 0 us
  waiting for transfers between devices: 5.52 us -> 6.19 us
    all_to_all x1, waiting for transfers between devices: 1.65 us -> 6.18 us  [per_device(): chunks = lax.all_to_all(chunks, ('gx', 'gy'), 0, 0)]
    ppermute x1, waiting for transfers between devices: 3.86 us -> 0.01 us  [per_device(): second = lax.ppermute(second, 'gx', far)]
    all_to_all x1, starting transfers between devices: 7.3 us -> 3.97 us  [per_device(): chunks = lax.all_to_all(chunks, ('gx', 'gy'), 0, 0)]
    pallas_call x2 -> x3, Pallas kernels: 3.95 us -> 5.91 us  [the longest x1 2.42 us: per_device(): pl.pallas_call(functools.partial(pack_kernel, gx, gy), in_specs=[any_plac...]
    unnamed x14 -> x0, local copies, waits for them, and re-layouts: 1.07 us -> none
    ppermute x1, starting transfers between devices: 2.53 us -> 3.56 us  [per_device(): second = lax.ppermute(second, 'gx', far)]
  transfers between devices with their start and end apart: 3 -> 3, of which waited for: 2 -> 1; matrix products, arithmetic and copies ran while one was open for 0% -> 0% of each run, Pallas kernels for 0% -> 11%
where the time goes in v1:
time: 21.1 us; the launch traced here: 20.8 us
  starting transfers between devices  8.05 us (38%)
  waiting for transfers between devices  6.19 us (29%)
  Pallas kernels  5.91 us (28%)
  between operations  0.67 us (3%)
    all_to_all x1, waiting for transfers between devices, per_device(): chunks = lax.all_to_all(chunks, ('gx', 'gy'), 0, 0)  6.18 us
    all_to_all x1, starting transfers between devices, per_device(): chunks = lax.all_to_all(chunks, ('gx', 'gy'), 0, 0)  3.97 us
    ppermute x1, starting transfers between devices, per_device(): second = lax.ppermute(second, 'gx', far)  3.56 us
    pallas_call x1, Pallas kernels, per_device(): pl.pallas_call(functools.partial(pack_kernel, gx, gy), in_specs=[any_plac...  2.42 us
    pallas_call x1, Pallas kernels, per_device(): pl.pallas_call(interior_kernel, in_specs=[on_chip] * 4 + [any_place], out...  2.19 us
    pallas_call x1, Pallas kernels, per_device(): pl.pallas_call(functools.partial(finish_kernel, gx, gy), in_specs=[on_chi...  1.3 us
    ppermute x1, starting transfers between devices, per_device(): first = lax.ppermute(first, 'gx', near)  0.52 us
  transfers between devices with their start and end apart: 3, of which 1 were waited for; matrix products, arithmetic and copies ran while one was open for 0% of the time, Pallas kernels for 11%

profile of v1, /device:TPU:0, one launch (start us, length us, event | category | flops | bytes accessed | tf_op | source)
XLA Modules:
  0.0 20.8 jit_solution(5647718005186631711)
XLA Ops:
  0.6 2.4 %pack.1 = (f32[4,4,64,128]{3,2,1,0:T(8,128)S(1)}, f32[4,4,64,128]{3,2,1,0:T(8,128)S(1)}, f32[4,128]{1,0:T(4,128)S(1)}, s32[4,128]{1,0:T(4,128)S(1)}, f32[192,128...) custom-call(f32[4,4,64,128]{3,2,1,0:T(8,128)} %bitcast.12, f32[4,4,64,128]{3,2,1,0:T(8,128)} %bitcast.13, ...), custom_call_target="tpu_custom_call" | custom-call | tf_op jit(solution)/shard_map/pack/pallas_call | solution.py:493
  3.1 0.5 %collective-permute-start = (f32[192,128]{1,0:T(8,128)S(1)}, f32[192,128]{1,0:T(8,128)S(1)}, u32[]{:S(2)}, u32[]{:S(2)}) collective-permute-start(f32[192,128]{1,0:T(8,128)S(1)} %get-tuple-element.25), channel_id=1, source_target_pairs={{0,4},{4,0},{8,12},{12,8},{16,20},{20,16},{24,28},{28,24},{1,5},{5... | collective-permute-start | bytes 294920 | tf_op jit(solution)/shard_map/ppermute | solution.py:516
  3.6 3.6 %collective-permute-start.1 = (f32[192,128]{1,0:T(8,128)S(1)}, f32[192,128]{1,0:T(8,128)S(1)}, u32[]{:S(2)}, u32[]{:S(2)}) collective-permute-start(f32[192,128]{1,0:T(8,128)S(1)} %get-tuple-element.26), channel_id=1, source_target_pairs={{0,28},{4,8},{8,4},{12,16},{16,12},{20,24},{24,20},{28,0},{1,29},{... | collective-permute-start | bytes 294920 | tf_op jit(solution)/shard_map/ppermute | solution.py:517
  7.1 4.0 %all-to-all-start = ((f32[32,8,128]{2,1,0:T(8,128)}), f32[32,8,128]{2,1,0:T(8,128)S(1)}, u32[]{:S(2)}, u32[]{:S(2)}) async-start(f32[32,8,128]{2,1,0:T(8,128)} %get-tuple-element.30), calls=%async_computation | async-start | bytes 262144 | tf_op jit(solution)/shard_map/all_to_all | solution.py:518
  11.1 0.0 collective-permute-done.first
  11.1 0.0 collective-permute-done.1.second
  11.1 2.2 %interior.1 = (f32[4,4,64,128]{3,2,1,0:T(8,128)S(1)}, f32[4,4,64,128]{3,2,1,0:T(8,128)S(1)}, f32[4,4,64,128]{3,2,1,0:T(8,128)S(1)}, f32[4,4,64,128]{3,2,1,0:T(8,...) custom-call(f32[4,4,64,128]{3,2,1,0:T(8,128)S(1)} %get-tuple-element.21.st, ...), custom_call_target="tpu_custom_call" | custom-call | flops 30000001024 | bytes 2400000 | tf_op jit(solution)/shard_map/interior/pallas_call | solution.py:520
  13.3 6.2 %all-to-all-done.chunks = f32[32,8,128]{2,1,0:T(8,128)S(1)} async-done(((f32[32,8,128]{2,1,0:T(8,128)}), f32[32,8,128]{2,1,0:T(8,128)S(1)}, u32[]{:S(2)}, u32[]{:S(2)}) %all-to-all-start) | async-done | bytes 131104 | tf_op jit(solution)/shard_map/all_to_all | solution.py:518
  19.5 1.3 %finish.1 = (f32[4,4,64,128]{3,2,1,0:T(8,128)}, f32[4,4,64,128]{3,2,1,0:T(8,128)}, f32[4,4,64,128]{3,2,1,0:T(8,128)}, f32[4,128]{1,0:T(4,128)}) custom-call(f32[4,4,64,128]{3,2,1,0:T(8,128)S(1)} %get-tuple-element.21.st, f32[4,4,64,128]{3,2,1,0:T(8,128)S(1)} %get-tuple-element.22.ct, ...), custom_call_target="tpu_custom_call", output_to_operand_aliasing={{0}: (8, {}), {1}: (9, {}), {2}: (10, {})} | custom-call | tf_op jit(solution)/shard_map/finish/pallas_call | solution.py:532
Async XLA Ops:
  3.1 8.1 %collective-permute-start = (f32[192,128]{1,0:T(8,128)S(1)}, f32[192,128]{1,0:T(8,128)S(1)}, u32[]{:S(2)}, u32[]{:S(2)}) collective-permute-start(f32[192,128]{1,0:T(8,128)S(1)} %get-tuple-element.25), channel_id=1, source_target_pairs={{0,4},{4,0},{8,12},{12,8},{16,20},{20,16},{24,28},{28,24},{1,5},{5... | collective-permute-start | bytes 294920 | tf_op jit(solution)/shard_map/ppermute | solution.py:516
  3.6 7.5 %collective-permute-start.1 = (f32[192,128]{1,0:T(8,128)S(1)}, f32[192,128]{1,0:T(8,128)S(1)}, u32[]{:S(2)}, u32[]{:S(2)}) collective-permute-start(f32[192,128]{1,0:T(8,128)S(1)} %get-tuple-element.26), channel_id=1, source_target_pairs={{0,28},{4,8},{8,4},{12,16},{16,12},{20,24},{24,20},{28,0},{1,29},{... | collective-permute-start | bytes 294920 | tf_op jit(solution)/shard_map/ppermute | solution.py:517
  7.1 12.4 %all-to-all-start = ((f32[32,8,128]{2,1,0:T(8,128)}), f32[32,8,128]{2,1,0:T(8,128)S(1)}, u32[]{:S(2)}, u32[]{:S(2)}) async-start(f32[32,8,128]{2,1,0:T(8,128)} %get-tuple-element.30), calls=%async_computation | async-start | bytes 262144 | tf_op jit(solution)/shard_map/all_to_all | solution.py:518

commit v2 on v1

--- a/solution.py
+++ b/solution.py
@@ -15,9 +15,7 @@
 lift_half = 6.0
 
 LANES = 128
-HALO_LANES = 48
-IMP_LANE = 48
-SUM_LANE = 64
+ROWS = 5
 
 
 def derivative_table():
@@ -74,37 +72,57 @@
 
 
 def pack_kernel(
-    gx, gy, st_in, ct_in, imp_in, wp_in, st, ct, imp, wp, first, second, chunks, sems, small, one_hot
+    gx,
+    gy,
+    st_in,
+    ct_in,
+    imp_in,
+    wp_in,
+    st,
+    ct,
+    imp,
+    wp,
+    first,
+    second,
+    third,
+    fourth,
+    chunks_out,
+    chunks,
+    one_hot,
+    sems,
+    small,
 ):
     me_x, me_y = lax.axis_index("gx"), lax.axis_index("gy")
     rows, lanes = rows_iota(), lanes_iota()
     even_row = (rows & 1) == 0
     even_me = (me_x & 1) == 0
+    load_wp = pltpu.make_async_copy(wp_in, wp, small.at[0])
+    load_wp.start()
     loads = {}
-    for number, (source, target) in enumerate(((imp_in, imp), (wp_in, wp))):
-        loads[number, 4] = pltpu.make_async_copy(source, target, small.at[number])
-    loads[1, 4].start()
-    for a in (0, 3, 1, 2):
+    for field in (0, 3, 2, 1):
         for number, (source, target) in enumerate(((st_in, st), (ct_in, ct))):
-            loads[number, a] = pltpu.make_async_copy(
-                source.at[:, a], target.at[:, a], sems.at[number, a]
+            loads[number, field] = pltpu.make_async_copy(
+                source.at[field], target.at[field], sems.at[number, field]
             )
-            loads[number, a].start()
-    loads[0, 4].start()
-    up = jnp.zeros((8, LANES), jnp.float32)
-    down = jnp.zeros((8, LANES), jnp.float32)
+            loads[number, field].start()
+    load_imp = pltpu.make_async_copy(imp_in, imp, small.at[1])
+    load_imp.start()
+
+    load_wp.wait()
+    groups = 4 * gy
+    count = 4 * LANES
+    patch = jnp.concatenate([wp[r : r + 1, :] for r in range(4)], axis=1)
+    high_of = lax.shift_right_logical(patch, 7)
+    low_of = patch & (LANES - 1)
+    hot = lax.broadcasted_iota(jnp.int32, (LANES, count), 0) == low_of
+    one_hot[...] = jnp.where(hot, 1.0, 0.0).astype(jnp.bfloat16)
+
+    for field in (0, 3):
+        for number in range(2):
+            loads[number, field].wait()
     floor = jnp.zeros((8, LANES), jnp.float32)
     ceil = jnp.zeros((8, LANES), jnp.float32)
-
-    def columns_and_walls(a, up, down, floor, ceil):
-        for number, (ref, sigma) in enumerate(((st, 1), (ct, -1))):
-            for half in range(2):
-                high = y_trace(ref, sigma, a, 3, half)
-                low = y_trace(ref, sigma, a, 0, half)
-                for part in range(3):
-                    k = (number * 3 + part) * 8 + a * 2 + half
-                    up = jnp.where(lanes == k, lane_roll(high[part], k - 127), up)
-                    down = jnp.where(lanes == k, lane_roll(low[part], k), down)
+    for a in range(4):
         for b in range(4):
             floor += (load(st, 0, a, b, 0) - load(st, 3, a, b, 0)) * (
                 load(ct, 0, a, b, 0) + load(ct, 3, a, b, 0)
@@ -112,37 +130,6 @@
             ceil += (load(st, 0, a, b, 1) + load(st, 3, a, b, 1)) * (
                 load(ct, 0, a, b, 1) - load(ct, 3, a, b, 1)
             )
-        return up, down, floor, ceil
-
-    loads[1, 4].wait()
-    groups = 4 * gy
-    count = 4 * LANES
-    patch = jnp.concatenate([wp[r : r + 1, :] for r in range(4)], axis=1)
-    high_of = lax.shift_right_logical(patch, 7)
-    low_of = patch & (LANES - 1)
-    hot = lax.broadcasted_iota(jnp.int32, (LANES, count), 0) == low_of
-    one_hot[...] = jnp.where(hot, 1.0, 0.0).astype(jnp.bfloat16)
-    loads[0, 0].wait()
-    loads[1, 0].wait()
-    up, down, floor, ceil = columns_and_walls(0, up, down, floor, ceil)
-    loads[0, 3].wait()
-    loads[1, 3].wait()
-    up, down, floor, ceil = columns_and_walls(3, up, down, floor, ceil)
-    for number, (ref, sigma) in enumerate(((st, 1), (ct, -1))):
-        for b in range(4):
-            high = [x_trace(ref, sigma, 3, b, half) for half in range(2)]
-            low = [x_trace(ref, sigma, 0, b, half) for half in range(2)]
-            for part in range(3):
-                to_right = jnp.where(even_row, sub_roll(high[0][part], -1), high[1][part])
-                to_left = jnp.where(even_row, low[1][part], sub_roll(low[0][part], 1))
-                at = pl.ds(((number * 3 + part) * 4 + b) * 8, 8)
-                first[at, :] = jnp.where(even_me, to_right, to_left)
-                second[at, :] = jnp.where(even_me, to_left, to_right)
-    for a in (1, 2):
-        loads[0, a].wait()
-        loads[1, a].wait()
-        up, down, floor, ceil = columns_and_walls(a, up, down, floor, ceil)
-    loads[0, 4].wait()
     values = jnp.concatenate([floor[0:1], floor[1:2], ceil[6:7], ceil[7:8]], axis=1)
     chosen = lax.broadcasted_iota(jnp.int32, (groups, count), 0) == high_of
     spread = jnp.where(chosen, jnp.broadcast_to(values, (groups, count)), 0.0)
@@ -155,30 +142,49 @@
         pieces, one_hot[...], (((1,), (1,)), ((), ())), preferred_element_type=jnp.float32
     )
     sums = sums[:groups] + sums[groups : 2 * groups] + sums[2 * groups :]
-    width = LANES // gx
-    shard = jnp.concatenate([imp[...], imp[...]], axis=0)
-    placed = pltpu.roll(shard, (IMP_LANE - me_x * width + LANES) % LANES, 1)
-    odd_me_y = me_y & 1
-    imp_here = (
-        (lanes >= IMP_LANE)
-        & (lanes < IMP_LANE + width)
-        & (lax.shift_right_logical(rows, 2) == odd_me_y)
-    )
-    common = jnp.where(imp_here, placed, 0.0)
-    upper_lanes = lanes >= SUM_LANE
-    tiles = []
+    load_imp.wait()
+    width = LANES * 4 // gx
+    per_row = gx // 4
+    line = imp[pl.ds(me_x // per_row, 1), :]
+    place = lax.rem(me_x, per_row)
+    line_lanes = lax.broadcasted_iota(jnp.int32, (1, LANES), 1)
+    line = jnp.where(line_lanes // width == place, line, 0.0)
     for target in range(gy):
-        part = sums[target * 4 : target * 4 + 4]
-        both = jnp.concatenate([pltpu.roll(part, SUM_LANE, 1), part], axis=0)
-        tiles.append(jnp.where(upper_lanes, both, common))
-    for x in range(gx):
-        for target in range(gy):
-            chunks[x * gy + target] = tiles[target]
-    halo_lanes = lanes < HALO_LANES
-    next_y = me_x * gy + lax.rem(me_y + 1, gy)
-    prev_y = me_x * gy + lax.rem(me_y + gy - 1, gy)
-    chunks[next_y] = jnp.where(halo_lanes, up, chunks[next_y])
-    chunks[prev_y] = jnp.where(halo_lanes, down, chunks[prev_y])
+        tile = jnp.concatenate([sums[target * 4 : target * 4 + 4], line], axis=0)
+        for x in range(gx):
+            chunks[pl.ds((x * gy + target) * ROWS, ROWS), :] = tile
+    send = pltpu.make_async_copy(chunks, chunks_out, small.at[2])
+    send.start()
+
+    for field in (2, 1):
+        for number in range(2):
+            loads[number, field].wait()
+    up = jnp.zeros((8, LANES), jnp.float32)
+    down = jnp.zeros((8, LANES), jnp.float32)
+    for number, (ref, sigma) in enumerate(((st, 1), (ct, -1))):
+        for a in range(4):
+            for half in range(2):
+                high = y_trace(ref, sigma, a, 3, half)
+                low = y_trace(ref, sigma, a, 0, half)
+                for part in range(3):
+                    k = (number * 3 + part) * 8 + a * 2 + half
+                    up = jnp.where(lanes == k, lane_roll(high[part], k - 127), up)
+                    down = jnp.where(lanes == k, lane_roll(low[part], k), down)
+    even_me_y = (me_y & 1) == 0
+    third[...] = jnp.where(even_me_y, up, down)
+    fourth[...] = jnp.where(even_me_y, down, up)
+
+    for number, (ref, sigma) in enumerate(((st, 1), (ct, -1))):
+        for b in range(4):
+            high = [x_trace(ref, sigma, 3, b, half) for half in range(2)]
+            low = [x_trace(ref, sigma, 0, b, half) for half in range(2)]
+            for part in range(3):
+                to_right = jnp.where(even_row, sub_roll(high[0][part], -1), high[1][part])
+                to_left = jnp.where(even_row, low[1][part], sub_roll(low[0][part], 1))
+                at = pl.ds(((number * 3 + part) * 4 + b) * 8, 8)
+                first[at, :] = jnp.where(even_me, to_right, to_left)
+                second[at, :] = jnp.where(even_me, to_left, to_right)
+    send.wait()
 
 
 def interior(ref, sigma, matrix, scale, x_low, x_high, emit):
@@ -361,6 +367,8 @@
     new_rg,
     grad,
     chunks,
+    third,
+    fourth,
     st_prior,
     rg_prior,
     grad_prior,
@@ -377,7 +385,7 @@
     last_sem,
 ):
     del st_prior, rg_prior, grad_prior
-    me_x, me_y = lax.axis_index("gx"), lax.axis_index("gy")
+    me_y = lax.axis_index("gy")
     rows, lanes = rows_iota(), lanes_iota()
     stores = []
 
@@ -395,20 +403,19 @@
                 at = (pl.ds(field, 1), every, pl.ds(16, 32))
                 store(source, target, at, kind, piece)
 
-    width = LANES // gx
     total = None
-    for group in range(gy // 2):
-        block = jnp.zeros((8, LANES), jnp.float32)
-        for x in range(gx):
-            pair = chunks[x * gy + 2 * group] + chunks[x * gy + 2 * group + 1]
-            total = pair if total is None else total + pair
-            moved = lane_roll(pair, x * width - IMP_LANE)
-            here = (lanes >= x * width) & (lanes < (x + 1) * width)
-            block = jnp.where(here, moved, block)
-        table[group * 8 : group * 8 + 8, :] = (block - 1.0) / (block + 1.0)
-    patch_sum = jnp.where(
-        lanes < SUM_LANE, pltpu.roll(total, SUM_LANE, 1), sub_roll(total, 4)
-    )[:4]
+    per_row = gx // 4
+    for y in range(gy):
+        for quarter in range(4):
+            parts = []
+            for x in range(quarter * per_row, (quarter + 1) * per_row):
+                start = (x * gy + y) * ROWS
+                piece = chunks[start : start + 4, :]
+                total = piece if total is None else total + piece
+                parts.append(chunks[start + 4 : start + 5, :])
+            line = functools.reduce(jnp.add, parts)
+            table[y * 4 + quarter : y * 4 + quarter + 1, :] = (line - 1.0) / (line + 1.0)
+    patch_sum = total
     above = imp[...] + 1.0
     factor = time_step * section_b * lift_half * 2.0
     imp_grad[...] = patch_sum * jnp.float32(factor) / (above * above)
@@ -423,8 +430,9 @@
         found = jnp.take_along_axis(line, low_of, axis=1)
         reflect = jnp.where(high_of == high, found, reflect)
 
-    below = chunks[me_x * gy + lax.rem(me_y + gy - 1, gy)]
-    ahead = chunks[me_x * gy + lax.rem(me_y + 1, gy)]
+    even_me_y = (me_y & 1) == 0
+    below = jnp.where(even_me_y, fourth[...], third[...])
+    ahead = jnp.where(even_me_y, third[...], fourth[...])
 
     for number, ref, sigma, scale in (
         (1, ct, -1, time_step * section_b),
@@ -490,10 +498,11 @@
     whole = pltpu.VMEM(flat, f32)
     params = pltpu.CompilerParams(vmem_limit_bytes=8 * 2**20)
     halo = pltpu.VMEM((192, LANES), f32)
-    st, ct, imp, wp, first, second, chunks = pl.pallas_call(
+    column = pltpu.VMEM((8, LANES), f32)
+    st, ct, imp, wp, first, second, third, fourth, chunks = pl.pallas_call(
         functools.partial(pack_kernel, gx, gy),
         in_specs=[any_place] * 4,
-        out_specs=[on_chip] * 7,
+        out_specs=[on_chip] * 8 + [any_place],
         out_shape=(
             whole,
             whole,
@@ -501,21 +510,33 @@
             pltpu.VMEM((4, LANES), jnp.int32),
             halo,
             halo,
-            pltpu.VMEM((gx * gy, 8, LANES), f32),
+            column,
+            column,
+            pltpu.HBM((gx * gy * ROWS, LANES), f32),
         ),
         scratch_shapes=[
+            pltpu.VMEM((gx * gy * ROWS, LANES), f32),
+            pltpu.VMEM((LANES, 4 * LANES), jnp.bfloat16),
             pltpu.SemaphoreType.DMA((2, 4)),
-            pltpu.SemaphoreType.DMA((2,)),
-            pltpu.VMEM((LANES, 4 * LANES), jnp.bfloat16),
+            pltpu.SemaphoreType.DMA((3,)),
         ],
         compiler_params=params,
         name="pack",
     )(*(pltpu.with_memory_space_constraint(v, pltpu.HBM) for v in (st, ct, imp, wp)))
-    near = [(i, i ^ 1) for i in range(gx)]
-    far = [(i, (i + 1) % gx if i % 2 else (i - 1) % gx) for i in range(gx)]
-    first = lax.ppermute(first, "gx", near)
-    second = lax.ppermute(second, "gx", far)
-    chunks = lax.all_to_all(chunks, ("gx", "gy"), 0, 0)
+
+    def near(count):
+        return [(i, i ^ 1) for i in range(count)]
+
+    def far(count):
+        return [(i, (i + 1) % count if i % 2 else (i - 1) % count) for i in range(count)]
+
+    first = lax.ppermute(first, "gx", near(gx))
+    second = lax.ppermute(second, "gx", far(gx))
+    chunks = lax.all_to_all(
+        chunks.reshape(gx * gy, ROWS, 1, LANES), ("gx", "gy"), 0, 0
+    ).reshape(gx * gy * ROWS, LANES)
+    third = lax.ppermute(third, "gy", near(gy))
+    fourth = lax.ppermute(fourth, "gy", far(gy))
     result = pltpu.HBM(flat, f32)
     new_st, new_rg, grad, st_out, rg_out, grad_out = pl.pallas_call(
         interior_kernel,
@@ -531,10 +552,10 @@
     )(st, ct, first, second, pltpu.with_memory_space_constraint(rg, pltpu.HBM))
     new_st, new_rg, grad, imp_grad = pl.pallas_call(
         functools.partial(finish_kernel, gx, gy),
-        in_specs=[on_chip] * 8 + [any_place] * 3,
+        in_specs=[on_chip] * 10 + [any_place] * 3,
         out_specs=[any_place] * 4,
         out_shape=(result, result, result, pltpu.HBM((4, LANES), f32)),
-        input_output_aliases={8: 0, 9: 1, 10: 2},
+        input_output_aliases={10: 0, 11: 1, 12: 2},
         scratch_shapes=[
             pltpu.VMEM((4 * gy, LANES), f32),
             pltpu.VMEM((4, LANES), f32),
@@ -546,7 +567,21 @@
         ],
         compiler_params=params,
         name="finish",
-    )(st, ct, imp, wp, new_st, new_rg, grad, chunks, st_out, rg_out, grad_out)
+    )(
+        st,
+        ct,
+        imp,
+        wp,
+        new_st,
+        new_rg,
+        grad,
+        chunks,
+        third,
+        fourth,
+        st_out,
+        rg_out,
+        grad_out,
+    )
     return (
         new_st.reshape(state.shape),
         new_rg.reshape(state.shape),

time: 21.1 us -> 20 us (0.948)
  waiting for transfers between devices: 6.19 us -> 1.35 us
  starting transfers between devices: 8.05 us -> 12.2 us
  Pallas kernels: 5.91 us -> 5.47 us
    all_to_all x1, waiting for transfers between devices: 6.18 us -> 0.51 us  [per_device(): lax.all_to_all(chunks.reshape(gx * gy, ROWS, 1, LANES), ('gx', 'gy'), 0, 0)]
    ppermute x2 -> x4, starting transfers between devices: 4.08 us -> 8.28 us  [the longest x1 3.56 us: per_device(): second = lax.ppermute(second, 'gx', far(gx))]
    ppermute x2 -> x4, waiting for transfers between devices: 0.01 us -> 0.83 us  [the longest x1 0.82 us: per_device(): fourth = lax.ppermute(fourth, 'gy', far(gy))]
    pallas_call x1, Pallas kernels: 2.42 us -> 2.01 us  [per_device(): pl.pallas_call(functools.partial(pack_kernel, gx, gy), in_specs=[any_plac...]
  transfers between devices with their start and end apart: 3 -> 5, of which waited for: 1 -> 2; matrix products, arithmetic and copies ran while one was open for 0% -> 0% of each run, Pallas kernels for 11% -> 11%
where the time goes in v2:
time: 20 us; the launch traced here: 19.7 us
  starting transfers between devices  12.2 us (61%)
  Pallas kernels  5.47 us (27%)
  waiting for transfers between devices  1.35 us (7%)
  between operations  0.67 us (3%)
    all_to_all x1, starting transfers between devices, per_device(): lax.all_to_all(chunks.reshape(gx * gy, ROWS, 1, LANES), ('gx', 'gy'), 0, 0)  3.97 us
    ppermute x1, starting transfers between devices, per_device(): second = lax.ppermute(second, 'gx', far(gx))  3.56 us
    ppermute x1, starting transfers between devices, per_device(): fourth = lax.ppermute(fourth, 'gy', far(gy))  2.37 us
    pallas_call x1, Pallas kernels, per_device(): pl.pallas_call(interior_kernel, in_specs=[on_chip] * 4 + [any_place], out...  2.19 us
    pallas_call x1, Pallas kernels, per_device(): pl.pallas_call(functools.partial(pack_kernel, gx, gy), in_specs=[any_plac...  2.01 us
    ppermute x1, starting transfers between devices, per_device(): third = lax.ppermute(third, 'gy', near(gy))  1.84 us
    pallas_call x1, Pallas kernels, per_device(): pl.pallas_call(functools.partial(finish_kernel, gx, gy), in_specs=[on_chi...  1.27 us
    ppermute x1, waiting for transfers between devices, per_device(): fourth = lax.ppermute(fourth, 'gy', far(gy))  0.82 us
  transfers between devices with their start and end apart: 5, of which 2 were waited for; matrix products, arithmetic and copies ran while one was open for 0% of the time, Pallas kernels for 11%

profile of v2, /device:TPU:0, one launch (start us, length us, event | category | flops | bytes accessed | tf_op | source)
XLA Modules:
  0.0 19.7 jit_solution(12714908724387524728)
XLA Ops:
  0.6 2.0 %pack.1 = (f32[4,4,64,128]{3,2,1,0:T(8,128)S(1)}, f32[4,4,64,128]{3,2,1,0:T(8,128)S(1)}, f32[4,128]{1,0:T(4,128)S(1)}, s32[4,128]{1,0:T(4,128)S(1)}, f32[192,128...) custom-call(f32[4,4,64,128]{3,2,1,0:T(8,128)} %bitcast.15, ...), custom_call_target="tpu_custom_call" | custom-call | tf_op jit(solution)/shard_map/pack/pallas_call | solution.py:502
  2.6 0.5 %collective-permute-start = (f32[192,128]{1,0:T(8,128)S(1)}, f32[192,128]{1,0:T(8,128)S(1)}, u32[]{:S(2)}, u32[]{:S(2)}) collective-permute-start(f32[192,128]{1,0:T(8,128)S(1)} %get-tuple-element.27), channel_id=1, source_target_pairs={{0,4},{4,0},{8,12},{12,8},{16,20},{20,16},{24,28},{28,24},{1,5},{5... | collective-permute-start | bytes 294920 | tf_op jit(solution)/shard_map/ppermute | solution.py:533
  3.2 3.6 %collective-permute-start.1 = (f32[192,128]{1,0:T(8,128)S(1)}, f32[192,128]{1,0:T(8,128)S(1)}, u32[]{:S(2)}, u32[]{:S(2)}) collective-permute-start(f32[192,128]{1,0:T(8,128)S(1)} %get-tuple-element.28), channel_id=1, source_target_pairs={{0,28},{4,8},{8,4},{12,16},{16,12},{20,24},{24,20},{28,0},{1,29},{... | collective-permute-start | bytes 294920 | tf_op jit(solution)/shard_map/ppermute | solution.py:534
  6.7 4.0 %all-to-all-start = ((f32[32,5,1,128]{3,2,1,0:T(1,128)}), f32[32,5,1,128]{3,2,1,0:T(1,128)S(1)}, u32[]{:S(2)}, u32[]{:S(2)}) async-start(f32[32,5,1,128]{3,2,1,0:T(1,128)} %bitcast.17), calls=%async_computation | async-start | bytes 163840 | tf_op jit(solution)/shard_map/all_to_all | solution.py:535
  10.7 1.8 %collective-permute-start.2 = (f32[8,128]{1,0:T(8,128)S(1)}, f32[8,128]{1,0:T(8,128)S(1)}, u32[]{:S(2)}, u32[]{:S(2)}) collective-permute-start(f32[8,128]{1,0:T(8,128)S(1)} %get-tuple-element.33), channel_id=1, source_target_pairs={{0,1},{1,0},{2,3},{3,2},{4,5},{5,4},{6,7},{7,6},{8,9},{9,8},{10,11... | collective-permute-start | bytes 12296 | tf_op jit(solution)/shard_map/ppermute | solution.py:538
  12.5 2.4 %collective-permute-start.3 = (f32[8,128]{1,0:T(8,128)S(1)}, f32[8,128]{1,0:T(8,128)S(1)}, u32[]{:S(2)}, u32[]{:S(2)}) collective-permute-start(f32[8,128]{1,0:T(8,128)S(1)} %get-tuple-element.34), channel_id=1, source_target_pairs={{0,3},{1,2},{2,1},{3,0},{4,7},{5,6},{6,5},{7,4},{8,11},{9,10},{10,... | collective-permute-start | bytes 12296 | tf_op jit(solution)/shard_map/ppermute | solution.py:539
  14.9 0.0 collective-permute-done.first
  14.9 0.0 collective-permute-done.1.second
  14.9 2.2 %interior.1 = (f32[4,4,64,128]{3,2,1,0:T(8,128)S(1)}, f32[4,4,64,128]{3,2,1,0:T(8,128)S(1)}, f32[4,4,64,128]{3,2,1,0:T(8,128)S(1)}, f32[4,4,64,128]{3,2,1,0:T(8,...) custom-call(f32[4,4,64,128]{3,2,1,0:T(8,128)S(1)} %get-tuple-element.23.st, ...), custom_call_target="tpu_custom_call" | custom-call | flops 30000001024 | bytes 2400000 | tf_op jit(solution)/shard_map/interior/pallas_call | solution.py:541
  17.1 0.0 collective-permute-done.2.third
  17.1 0.8 %collective-permute-done.3.fourth = f32[8,128]{1,0:T(8,128)S(1)} collective-permute-done((f32[8,128]{1,0:T(8,128)S(1)}, f32[8,128]{1,0:T(8,128)S(1)}, u32[]{:S(2)}, u32[]{:S(2)}) %collective-permute-start.3) | collective-permute-done | bytes 4128 | tf_op jit(solution)/shard_map/ppermute | solution.py:539
  17.9 0.5 %all-to-all-done = f32[32,5,1,128]{3,2,1,0:T(1,128)S(1)} async-done(((f32[32,5,1,128]{3,2,1,0:T(1,128)}), f32[32,5,1,128]{3,2,1,0:T(1,128)S(1)}, u32[]{:S(2)}, u32[]{:S(2)}) %all-to-all-start) | async-done | bytes 81952 | tf_op jit(solution)/shard_map/all_to_all | solution.py:535
  18.5 1.3 %finish.1 = (f32[4,4,64,128]{3,2,1,0:T(8,128)}, f32[4,4,64,128]{3,2,1,0:T(8,128)}, f32[4,4,64,128]{3,2,1,0:T(8,128)}, f32[4,128]{1,0:T(4,128)}) custom-call(f32[4,4,64,128]{3,2,1,0:T(8,128)S(1)} %get-tuple-element.23.st, f32[4,4,64,128]{3,2,1,0:T(8,128)S(1)} %get-tuple-element.24.ct, ...), custom_call_target="tpu_custom_call", output_to_operand_aliasing={{0}: (10, {}), {1}: (11, {}), {2}: (12, {})} | custom-call | tf_op jit(solution)/shard_map/finish/pallas_call | solution.py:553
Async XLA Ops:
  2.6 12.3 %collective-permute-start = (f32[192,128]{1,0:T(8,128)S(1)}, f32[192,128]{1,0:T(8,128)S(1)}, u32[]{:S(2)}, u32[]{:S(2)}) collective-permute-start(f32[192,128]{1,0:T(8,128)S(1)} %get-tuple-element.27), channel_id=1, source_target_pairs={{0,4},{4,0},{8,12},{12,8},{16,20},{20,16},{24,28},{28,24},{1,5},{5... | collective-permute-start | bytes 294920 | tf_op jit(solution)/shard_map/ppermute | solution.py:533
  3.2 11.7 %collective-permute-start.1 = (f32[192,128]{1,0:T(8,128)S(1)}, f32[192,128]{1,0:T(8,128)S(1)}, u32[]{:S(2)}, u32[]{:S(2)}) collective-permute-start(f32[192,128]{1,0:T(8,128)S(1)} %get-tuple-element.28), channel_id=1, source_target_pairs={{0,28},{4,8},{8,4},{12,16},{16,12},{20,24},{24,20},{28,0},{1,29},{... | collective-permute-start | bytes 294920 | tf_op jit(solution)/shard_map/ppermute | solution.py:534
  6.7 11.7 %all-to-all-start = ((f32[32,5,1,128]{3,2,1,0:T(1,128)}), f32[32,5,1,128]{3,2,1,0:T(1,128)S(1)}, u32[]{:S(2)}, u32[]{:S(2)}) async-start(f32[32,5,1,128]{3,2,1,0:T(1,128)} %bitcast.17), calls=%async_computation | async-start | bytes 163840 | tf_op jit(solution)/shard_map/all_to_all | solution.py:535
  10.7 6.4 %collective-permute-start.2 = (f32[8,128]{1,0:T(8,128)S(1)}, f32[8,128]{1,0:T(8,128)S(1)}, u32[]{:S(2)}, u32[]{:S(2)}) collective-permute-start(f32[8,128]{1,0:T(8,128)S(1)} %get-tuple-element.33), channel_id=1, source_target_pairs={{0,1},{1,0},{2,3},{3,2},{4,5},{5,4},{6,7},{7,6},{8,9},{9,8},{10,11... | collective-permute-start | bytes 12296 | tf_op jit(solution)/shard_map/ppermute | solution.py:538
  12.5 5.4 %collective-permute-start.3 = (f32[8,128]{1,0:T(8,128)S(1)}, f32[8,128]{1,0:T(8,128)S(1)}, u32[]{:S(2)}, u32[]{:S(2)}) collective-permute-start(f32[8,128]{1,0:T(8,128)S(1)} %get-tuple-element.34), channel_id=1, source_target_pairs={{0,3},{1,2},{2,1},{3,0},{4,7},{5,6},{6,5},{7,4},{8,11},{9,10},{10,... | collective-permute-start | bytes 12296 | tf_op jit(solution)/shard_map/ppermute | solution.py:539

commit v3 on v2

--- a/solution.py
+++ b/solution.py
@@ -27,6 +27,15 @@
     matrix = matrix * (1.0 - identity)
     matrix = matrix - identity * matrix.sum(axis=1)[:, None]
     return 2.0 * matrix
+
+
+def group_order(gx, gy):
+    return list(range(gx * gy))[::-1]
+
+
+def slots_of(gx, gy):
+    order = group_order(gx, gy)
+    return [order.index(device) for device in range(gx * gy)]
 
 
 def rows_at(b, half):
@@ -110,6 +119,7 @@
 
     load_wp.wait()
     groups = 4 * gy
+    slots = slots_of(gx, gy)
     count = 4 * LANES
     patch = jnp.concatenate([wp[r : r + 1, :] for r in range(4)], axis=1)
     high_of = lax.shift_right_logical(patch, 7)
@@ -152,7 +162,7 @@
     for target in range(gy):
         tile = jnp.concatenate([sums[target * 4 : target * 4 + 4], line], axis=0)
         for x in range(gx):
-            chunks[pl.ds((x * gy + target) * ROWS, ROWS), :] = tile
+            chunks[pl.ds(slots[x * gy + target] * ROWS, ROWS), :] = tile
     send = pltpu.make_async_copy(chunks, chunks_out, small.at[2])
     send.start()
 
@@ -403,13 +413,14 @@
                 at = (pl.ds(field, 1), every, pl.ds(16, 32))
                 store(source, target, at, kind, piece)
 
+    slots = slots_of(gx, gy)
     total = None
     per_row = gx // 4
     for y in range(gy):
         for quarter in range(4):
             parts = []
             for x in range(quarter * per_row, (quarter + 1) * per_row):
-                start = (x * gy + y) * ROWS
+                start = slots[x * gy + y] * ROWS
                 piece = chunks[start : start + 4, :]
                 total = piece if total is None else total + piece
                 parts.append(chunks[start + 4 : start + 5, :])
@@ -533,7 +544,7 @@
     first = lax.ppermute(first, "gx", near(gx))
     second = lax.ppermute(second, "gx", far(gx))
     chunks = lax.all_to_all(
-        chunks.reshape(gx * gy, ROWS, 1, LANES), ("gx", "gy"), 0, 0
+        chunks.reshape(gx * gy, ROWS, 1, LANES), ("gx", "gy"), 0, 0, axis_index_groups=[group_order(gx, gy)]
     ).reshape(gx * gy * ROWS, LANES)
     third = lax.ppermute(third, "gy", near(gy))
     fourth = lax.ppermute(fourth, "gy", far(gy))

time: 20 us -> 19.6 us (0.980)
  waiting for transfers between devices: 1.35 us -> 1.01 us
    all_to_all x1, waiting for transfers between devices: 0.51 us -> 0.17 us  [per_device(): lax.all_to_all(chunks.reshape(gx * gy, ROWS, 1, LANES), ('gx', 'gy'), 0,...]
where the time goes in v3:
time: 19.6 us; the launch traced here: 19.4 us
  starting transfers between devices  12.2 us (62%)
  Pallas kernels  5.47 us (28%)
  waiting for transfers between devices  1.01 us (5%)
  between operations  0.67 us (3%)
    all_to_all x1, starting transfers between devices, per_device(): lax.all_to_all(chunks.reshape(gx * gy, ROWS, 1, LANES), ('gx', 'gy'), 0,...  3.97 us
    ppermute x1, starting transfers between devices, per_device(): second = lax.ppermute(second, 'gx', far(gx))  3.56 us
    ppermute x1, starting transfers between devices, per_device(): fourth = lax.ppermute(fourth, 'gy', far(gy))  2.37 us
    pallas_call x1, Pallas kernels, per_device(): pl.pallas_call(interior_kernel, in_specs=[on_chip] * 4 + [any_place], out...  2.19 us
    pallas_call x1, Pallas kernels, per_device(): pl.pallas_call(functools.partial(pack_kernel, gx, gy), in_specs=[any_plac...  2.01 us
    ppermute x1, starting transfers between devices, per_device(): third = lax.ppermute(third, 'gy', near(gy))  1.84 us
    pallas_call x1, Pallas kernels, per_device(): pl.pallas_call(functools.partial(finish_kernel, gx, gy), in_specs=[on_chi...  1.27 us
    ppermute x1, waiting for transfers between devices, per_device(): fourth = lax.ppermute(fourth, 'gy', far(gy))  0.82 us
  transfers between devices with their start and end apart: 5, of which 2 were waited for; matrix products, arithmetic and copies ran while one was open for 0% of the time, Pallas kernels for 11%

profile of v3, /device:TPU:0, one launch (start us, length us, event | category | flops | bytes accessed | tf_op | source)
XLA Modules:
  0.0 19.4 jit_solution(2660273762309131203)
XLA Ops:
  0.6 2.0 %pack.1 = (f32[4,4,64,128]{3,2,1,0:T(8,128)S(1)}, f32[4,4,64,128]{3,2,1,0:T(8,128)S(1)}, f32[4,128]{1,0:T(4,128)S(1)}, s32[4,128]{1,0:T(4,128)S(1)}, f32[192,128...) custom-call(f32[4,4,64,128]{3,2,1,0:T(8,128)} %bitcast.15, ...), custom_call_target="tpu_custom_call" | custom-call | tf_op jit(solution)/shard_map/pack/pallas_call | solution.py:513
  2.6 0.5 %collective-permute-start = (f32[192,128]{1,0:T(8,128)S(1)}, f32[192,128]{1,0:T(8,128)S(1)}, u32[]{:S(2)}, u32[]{:S(2)}) collective-permute-start(f32[192,128]{1,0:T(8,128)S(1)} %get-tuple-element.27), channel_id=1, source_target_pairs={{0,4},{4,0},{8,12},{12,8},{16,20},{20,16},{24,28},{28,24},{1,5},{5... | collective-permute-start | bytes 294920 | tf_op jit(solution)/shard_map/ppermute | solution.py:544
  3.2 3.6 %collective-permute-start.1 = (f32[192,128]{1,0:T(8,128)S(1)}, f32[192,128]{1,0:T(8,128)S(1)}, u32[]{:S(2)}, u32[]{:S(2)}) collective-permute-start(f32[192,128]{1,0:T(8,128)S(1)} %get-tuple-element.28), channel_id=1, source_target_pairs={{0,28},{4,8},{8,4},{12,16},{16,12},{20,24},{24,20},{28,0},{1,29},{... | collective-permute-start | bytes 294920 | tf_op jit(solution)/shard_map/ppermute | solution.py:545
  6.7 4.0 %all-to-all-start = ((f32[32,5,1,128]{3,2,1,0:T(1,128)}), f32[32,5,1,128]{3,2,1,0:T(1,128)S(1)}, u32[]{:S(2)}, u32[]{:S(2)}) async-start(f32[32,5,1,128]{3,2,1,0:T(1,128)} %bitcast.17), calls=%async_computation | async-start | bytes 163840 | tf_op jit(solution)/shard_map/all_to_all | solution.py:546
  10.7 1.8 %collective-permute-start.2 = (f32[8,128]{1,0:T(8,128)S(1)}, f32[8,128]{1,0:T(8,128)S(1)}, u32[]{:S(2)}, u32[]{:S(2)}) collective-permute-start(f32[8,128]{1,0:T(8,128)S(1)} %get-tuple-element.33), channel_id=1, source_target_pairs={{0,1},{1,0},{2,3},{3,2},{4,5},{5,4},{6,7},{7,6},{8,9},{9,8},{10,11... | collective-permute-start | bytes 12296 | tf_op jit(solution)/shard_map/ppermute | solution.py:549
  12.5 2.4 %collective-permute-start.3 = (f32[8,128]{1,0:T(8,128)S(1)}, f32[8,128]{1,0:T(8,128)S(1)}, u32[]{:S(2)}, u32[]{:S(2)}) collective-permute-start(f32[8,128]{1,0:T(8,128)S(1)} %get-tuple-element.34), channel_id=1, source_target_pairs={{0,3},{1,2},{2,1},{3,0},{4,7},{5,6},{6,5},{7,4},{8,11},{9,10},{10,... | collective-permute-start | bytes 12296 | tf_op jit(solution)/shard_map/ppermute | solution.py:550
  14.9 0.0 collective-permute-done.first
  14.9 0.0 collective-permute-done.1.second
  14.9 2.2 %interior.1 = (f32[4,4,64,128]{3,2,1,0:T(8,128)S(1)}, f32[4,4,64,128]{3,2,1,0:T(8,128)S(1)}, f32[4,4,64,128]{3,2,1,0:T(8,128)S(1)}, f32[4,4,64,128]{3,2,1,0:T(8,...) custom-call(f32[4,4,64,128]{3,2,1,0:T(8,128)S(1)} %get-tuple-element.23.st, ...), custom_call_target="tpu_custom_call" | custom-call | flops 30000001024 | bytes 2400000 | tf_op jit(solution)/shard_map/interior/pallas_call | solution.py:552
  17.1 0.0 collective-permute-done.2.third
  17.1 0.8 %collective-permute-done.3.fourth = f32[8,128]{1,0:T(8,128)S(1)} collective-permute-done((f32[8,128]{1,0:T(8,128)S(1)}, f32[8,128]{1,0:T(8,128)S(1)}, u32[]{:S(2)}, u32[]{:S(2)}) %collective-permute-start.3) | collective-permute-done | bytes 4128 | tf_op jit(solution)/shard_map/ppermute | solution.py:550
  17.9 0.2 all-to-all-done
  18.1 1.3 %finish.1 = (f32[4,4,64,128]{3,2,1,0:T(8,128)}, f32[4,4,64,128]{3,2,1,0:T(8,128)}, f32[4,4,64,128]{3,2,1,0:T(8,128)}, f32[4,128]{1,0:T(4,128)}) custom-call(f32[4,4,64,128]{3,2,1,0:T(8,128)S(1)} %get-tuple-element.23.st, f32[4,4,64,128]{3,2,1,0:T(8,128)S(1)} %get-tuple-element.24.ct, ...), custom_call_target="tpu_custom_call", output_to_operand_aliasing={{0}: (10, {}), {1}: (11, {}), {2}: (12, {})} | custom-call | tf_op jit(solution)/shard_map/finish/pallas_call | solution.py:564
Async XLA Ops:
  2.6 12.3 %collective-permute-start = (f32[192,128]{1,0:T(8,128)S(1)}, f32[192,128]{1,0:T(8,128)S(1)}, u32[]{:S(2)}, u32[]{:S(2)}) collective-permute-start(f32[192,128]{1,0:T(8,128)S(1)} %get-tuple-element.27), channel_id=1, source_target_pairs={{0,4},{4,0},{8,12},{12,8},{16,20},{20,16},{24,28},{28,24},{1,5},{5... | collective-permute-start | bytes 294920 | tf_op jit(solution)/shard_map/ppermute | solution.py:544
  3.2 11.7 %collective-permute-start.1 = (f32[192,128]{1,0:T(8,128)S(1)}, f32[192,128]{1,0:T(8,128)S(1)}, u32[]{:S(2)}, u32[]{:S(2)}) collective-permute-start(f32[192,128]{1,0:T(8,128)S(1)} %get-tuple-element.28), channel_id=1, source_target_pairs={{0,28},{4,8},{8,4},{12,16},{16,12},{20,24},{24,20},{28,0},{1,29},{... | collective-permute-start | bytes 294920 | tf_op jit(solution)/shard_map/ppermute | solution.py:545
  6.7 11.4 %all-to-all-start = ((f32[32,5,1,128]{3,2,1,0:T(1,128)}), f32[32,5,1,128]{3,2,1,0:T(1,128)S(1)}, u32[]{:S(2)}, u32[]{:S(2)}) async-start(f32[32,5,1,128]{3,2,1,0:T(1,128)} %bitcast.17), calls=%async_computation | async-start | bytes 163840 | tf_op jit(solution)/shard_map/all_to_all | solution.py:546
  10.7 6.4 %collective-permute-start.2 = (f32[8,128]{1,0:T(8,128)S(1)}, f32[8,128]{1,0:T(8,128)S(1)}, u32[]{:S(2)}, u32[]{:S(2)}) collective-permute-start(f32[8,128]{1,0:T(8,128)S(1)} %get-tuple-element.33), channel_id=1, source_target_pairs={{0,1},{1,0},{2,3},{3,2},{4,5},{5,4},{6,7},{7,6},{8,9},{9,8},{10,11... | collective-permute-start | bytes 12296 | tf_op jit(solution)/shard_map/ppermute | solution.py:549
  12.5 5.4 %collective-permute-start.3 = (f32[8,128]{1,0:T(8,128)S(1)}, f32[8,128]{1,0:T(8,128)S(1)}, u32[]{:S(2)}, u32[]{:S(2)}) collective-permute-start(f32[8,128]{1,0:T(8,128)S(1)} %get-tuple-element.34), channel_id=1, source_target_pairs={{0,3},{1,2},{2,1},{3,0},{4,7},{5,6},{6,5},{7,4},{8,11},{9,10},{10,... | collective-permute-start | bytes 12296 | tf_op jit(solution)/shard_map/ppermute | solution.py:550

commit v4 on v3

--- a/solution.py
+++ b/solution.py
@@ -107,6 +107,8 @@
     even_me = (me_x & 1) == 0
     load_wp = pltpu.make_async_copy(wp_in, wp, small.at[0])
     load_wp.start()
+    load_imp = pltpu.make_async_copy(imp_in, imp, small.at[1])
+    load_imp.start()
     loads = {}
     for field in (0, 3, 2, 1):
         for number, (source, target) in enumerate(((st_in, st), (ct_in, ct))):
@@ -114,8 +116,6 @@
                 source.at[field], target.at[field], sems.at[number, field]
             )
             loads[number, field].start()
-    load_imp = pltpu.make_async_copy(imp_in, imp, small.at[1])
-    load_imp.start()
 
     load_wp.wait()
     groups = 4 * gy
@@ -425,7 +425,7 @@
                 total = piece if total is None else total + piece
                 parts.append(chunks[start + 4 : start + 5, :])
             line = functools.reduce(jnp.add, parts)
-            table[y * 4 + quarter : y * 4 + quarter + 1, :] = (line - 1.0) / (line + 1.0)
+            table[y * 4 + quarter : y * 4 + quarter + 1, :] = line
     patch_sum = total
     above = imp[...] + 1.0
     factor = time_step * section_b * lift_half * 2.0
@@ -435,15 +435,16 @@
     patch = jnp.concatenate([wp[...], wp[...]], axis=0)
     low_of = patch & (LANES - 1)
     high_of = lax.shift_right_logical(patch, 7)
-    reflect = jnp.zeros((8, LANES), jnp.float32)
+    chosen = jnp.zeros((8, LANES), jnp.float32)
     for high in range(4 * gy):
         line = jnp.broadcast_to(table[high : high + 1, :], (8, LANES))
         found = jnp.take_along_axis(line, low_of, axis=1)
-        reflect = jnp.where(high_of == high, found, reflect)
+        chosen = jnp.where(high_of == high, found, chosen)
 
     even_me_y = (me_y & 1) == 0
     below = jnp.where(even_me_y, fourth[...], third[...])
     ahead = jnp.where(even_me_y, third[...], fourth[...])
+    reflect = (chosen - 1.0) / (chosen + 1.0)
 
     for number, ref, sigma, scale in (
         (1, ct, -1, time_step * section_b),

time: 19.6 us -> 19.6 us (level)
  no operation moved by 1% of the time
where the time goes in v4:
time: 19.6 us; the launch traced here: 19.4 us
  starting transfers between devices  12.2 us (62%)
  Pallas kernels  5.48 us (28%)
  waiting for transfers between devices  1.01 us (5%)
  between operations  0.67 us (3%)
    all_to_all x1, starting transfers between devices, per_device(): lax.all_to_all(chunks.reshape(gx * gy, ROWS, 1, LANES), ('gx', 'gy'), 0,...  3.97 us
    ppermute x1, starting transfers between devices, per_device(): second = lax.ppermute(second, 'gx', far(gx))  3.56 us
    ppermute x1, starting transfers between devices, per_device(): fourth = lax.ppermute(fourth, 'gy', far(gy))  2.37 us
    pallas_call x1, Pallas kernels, per_device(): pl.pallas_call(interior_kernel, in_specs=[on_chip] * 4 + [any_place], out...  2.19 us
    pallas_call x1, Pallas kernels, per_device(): pl.pallas_call(functools.partial(pack_kernel, gx, gy), in_specs=[any_plac...  2.01 us
    ppermute x1, starting transfers between devices, per_device(): third = lax.ppermute(third, 'gy', near(gy))  1.84 us
    pallas_call x1, Pallas kernels, per_device(): pl.pallas_call(functools.partial(finish_kernel, gx, gy), in_specs=[on_chi...  1.28 us
    ppermute x1, waiting for transfers between devices, per_device(): fourth = lax.ppermute(fourth, 'gy', far(gy))  0.82 us
  transfers between devices with their start and end apart: 5, of which 2 were waited for; matrix products, arithmetic and copies ran while one was open for 0% of the time, Pallas kernels for 11%

profile of v4, /device:TPU:0, one launch (start us, length us, event | category | flops | bytes accessed | tf_op | source)
XLA Modules:
  0.0 19.4 jit_solution(3516151402119477418)
XLA Ops:
  0.6 2.0 %pack.1 = (f32[4,4,64,128]{3,2,1,0:T(8,128)S(1)}, f32[4,4,64,128]{3,2,1,0:T(8,128)S(1)}, f32[4,128]{1,0:T(4,128)S(1)}, s32[4,128]{1,0:T(4,128)S(1)}, f32[192,128...) custom-call(f32[4,4,64,128]{3,2,1,0:T(8,128)} %bitcast.15, ...), custom_call_target="tpu_custom_call" | custom-call | tf_op jit(solution)/shard_map/pack/pallas_call | solution.py:514
  2.6 0.5 %collective-permute-start = (f32[192,128]{1,0:T(8,128)S(1)}, f32[192,128]{1,0:T(8,128)S(1)}, u32[]{:S(2)}, u32[]{:S(2)}) collective-permute-start(f32[192,128]{1,0:T(8,128)S(1)} %get-tuple-element.27), channel_id=1, source_target_pairs={{0,4},{4,0},{8,12},{12,8},{16,20},{20,16},{24,28},{28,24},{1,5},{5... | collective-permute-start | bytes 294920 | tf_op jit(solution)/shard_map/ppermute | solution.py:545
  3.2 3.6 %collective-permute-start.1 = (f32[192,128]{1,0:T(8,128)S(1)}, f32[192,128]{1,0:T(8,128)S(1)}, u32[]{:S(2)}, u32[]{:S(2)}) collective-permute-start(f32[192,128]{1,0:T(8,128)S(1)} %get-tuple-element.28), channel_id=1, source_target_pairs={{0,28},{4,8},{8,4},{12,16},{16,12},{20,24},{24,20},{28,0},{1,29},{... | collective-permute-start | bytes 294920 | tf_op jit(solution)/shard_map/ppermute | solution.py:546
  6.7 4.0 %all-to-all-start = ((f32[32,5,1,128]{3,2,1,0:T(1,128)}), f32[32,5,1,128]{3,2,1,0:T(1,128)S(1)}, u32[]{:S(2)}, u32[]{:S(2)}) async-start(f32[32,5,1,128]{3,2,1,0:T(1,128)} %bitcast.17), calls=%async_computation | async-start | bytes 163840 | tf_op jit(solution)/shard_map/all_to_all | solution.py:547
  10.7 1.8 %collective-permute-start.2 = (f32[8,128]{1,0:T(8,128)S(1)}, f32[8,128]{1,0:T(8,128)S(1)}, u32[]{:S(2)}, u32[]{:S(2)}) collective-permute-start(f32[8,128]{1,0:T(8,128)S(1)} %get-tuple-element.33), channel_id=1, source_target_pairs={{0,1},{1,0},{2,3},{3,2},{4,5},{5,4},{6,7},{7,6},{8,9},{9,8},{10,11... | collective-permute-start | bytes 12296 | tf_op jit(solution)/shard_map/ppermute | solution.py:550
  12.5 2.4 %collective-permute-start.3 = (f32[8,128]{1,0:T(8,128)S(1)}, f32[8,128]{1,0:T(8,128)S(1)}, u32[]{:S(2)}, u32[]{:S(2)}) collective-permute-start(f32[8,128]{1,0:T(8,128)S(1)} %get-tuple-element.34), channel_id=1, source_target_pairs={{0,3},{1,2},{2,1},{3,0},{4,7},{5,6},{6,5},{7,4},{8,11},{9,10},{10,... | collective-permute-start | bytes 12296 | tf_op jit(solution)/shard_map/ppermute | solution.py:551
  14.9 0.0 collective-permute-done.first
  14.9 0.0 collective-permute-done.1.second
  14.9 2.2 %interior.1 = (f32[4,4,64,128]{3,2,1,0:T(8,128)S(1)}, f32[4,4,64,128]{3,2,1,0:T(8,128)S(1)}, f32[4,4,64,128]{3,2,1,0:T(8,128)S(1)}, f32[4,4,64,128]{3,2,1,0:T(8,...) custom-call(f32[4,4,64,128]{3,2,1,0:T(8,128)S(1)} %get-tuple-element.23.st, ...), custom_call_target="tpu_custom_call" | custom-call | flops 30000001024 | bytes 2400000 | tf_op jit(solution)/shard_map/interior/pallas_call | solution.py:553
  17.1 0.0 collective-permute-done.2.third
  17.1 0.8 %collective-permute-done.3.fourth = f32[8,128]{1,0:T(8,128)S(1)} collective-permute-done((f32[8,128]{1,0:T(8,128)S(1)}, f32[8,128]{1,0:T(8,128)S(1)}, u32[]{:S(2)}, u32[]{:S(2)}) %collective-permute-start.3) | collective-permute-done | bytes 4128 | tf_op jit(solution)/shard_map/ppermute | solution.py:551
  17.9 0.2 all-to-all-done
  18.1 1.3 %finish.1 = (f32[4,4,64,128]{3,2,1,0:T(8,128)}, f32[4,4,64,128]{3,2,1,0:T(8,128)}, f32[4,4,64,128]{3,2,1,0:T(8,128)}, f32[4,128]{1,0:T(4,128)}) custom-call(f32[4,4,64,128]{3,2,1,0:T(8,128)S(1)} %get-tuple-element.23.st, f32[4,4,64,128]{3,2,1,0:T(8,128)S(1)} %get-tuple-element.24.ct, ...), custom_call_target="tpu_custom_call", output_to_operand_aliasing={{0}: (10, {}), {1}: (11, {}), {2}: (12, {})} | custom-call | tf_op jit(solution)/shard_map/finish/pallas_call | solution.py:565
Async XLA Ops:
  2.6 12.3 %collective-permute-start = (f32[192,128]{1,0:T(8,128)S(1)}, f32[192,128]{1,0:T(8,128)S(1)}, u32[]{:S(2)}, u32[]{:S(2)}) collective-permute-start(f32[192,128]{1,0:T(8,128)S(1)} %get-tuple-element.27), channel_id=1, source_target_pairs={{0,4},{4,0},{8,12},{12,8},{16,20},{20,16},{24,28},{28,24},{1,5},{5... | collective-permute-start | bytes 294920 | tf_op jit(solution)/shard_map/ppermute | solution.py:545
  3.2 11.7 %collective-permute-start.1 = (f32[192,128]{1,0:T(8,128)S(1)}, f32[192,128]{1,0:T(8,128)S(1)}, u32[]{:S(2)}, u32[]{:S(2)}) collective-permute-start(f32[192,128]{1,0:T(8,128)S(1)} %get-tuple-element.28), channel_id=1, source_target_pairs={{0,28},{4,8},{8,4},{12,16},{16,12},{20,24},{24,20},{28,0},{1,29},{... | collective-permute-start | bytes 294920 | tf_op jit(solution)/shard_map/ppermute | solution.py:546
  6.7 11.4 %all-to-all-start = ((f32[32,5,1,128]{3,2,1,0:T(1,128)}), f32[32,5,1,128]{3,2,1,0:T(1,128)S(1)}, u32[]{:S(2)}, u32[]{:S(2)}) async-start(f32[32,5,1,128]{3,2,1,0:T(1,128)} %bitcast.17), calls=%async_computation | async-start | bytes 163840 | tf_op jit(solution)/shard_map/all_to_all | solution.py:547
  10.7 6.4 %collective-permute-start.2 = (f32[8,128]{1,0:T(8,128)S(1)}, f32[8,128]{1,0:T(8,128)S(1)}, u32[]{:S(2)}, u32[]{:S(2)}) collective-permute-start(f32[8,128]{1,0:T(8,128)S(1)} %get-tuple-element.33), channel_id=1, source_target_pairs={{0,1},{1,0},{2,3},{3,2},{4,5},{5,4},{6,7},{7,6},{8,9},{9,8},{10,11... | collective-permute-start | bytes 12296 | tf_op jit(solution)/shard_map/ppermute | solution.py:550
  12.5 5.4 %collective-permute-start.3 = (f32[8,128]{1,0:T(8,128)S(1)}, f32[8,128]{1,0:T(8,128)S(1)}, u32[]{:S(2)}, u32[]{:S(2)}) collective-permute-start(f32[8,128]{1,0:T(8,128)S(1)} %get-tuple-element.34), channel_id=1, source_target_pairs={{0,3},{1,2},{2,1},{3,0},{4,7},{5,6},{6,5},{7,4},{8,11},{9,10},{10,... | collective-permute-start | bytes 12296 | tf_op jit(solution)/shard_map/ppermute | solution.py:551

commit v5 on v3

--- a/solution.py
+++ b/solution.py
@@ -30,7 +30,8 @@
 
 
 def group_order(gx, gy):
-    return list(range(gx * gy))[::-1]
+    first = list(range(gx * gy))[::-1]
+    return first[gx * gy // 2 :] + first[: gx * gy // 2]
 
 
 def slots_of(gx, gy):

time: 19.6 us -> 19.6 us (level)
  no operation moved by 1% of the time
where the time goes in v5:
time: 19.6 us; the launch traced here: 19.4 us
  starting transfers between devices  12.2 us (62%)
  Pallas kernels  5.47 us (28%)
  waiting for transfers between devices  1.01 us (5%)
  between operations  0.67 us (3%)
    all_to_all x1, starting transfers between devices, per_device(): lax.all_to_all(chunks.reshape(gx * gy, ROWS, 1, LANES), ('gx', 'gy'), 0,...  3.97 us
    ppermute x1, starting transfers between devices, per_device(): second = lax.ppermute(second, 'gx', far(gx))  3.56 us
    ppermute x1, starting transfers between devices, per_device(): fourth = lax.ppermute(fourth, 'gy', far(gy))  2.37 us
    pallas_call x1, Pallas kernels, per_device(): pl.pallas_call(interior_kernel, in_specs=[on_chip] * 4 + [any_place], out...  2.19 us
    pallas_call x1, Pallas kernels, per_device(): pl.pallas_call(functools.partial(pack_kernel, gx, gy), in_specs=[any_plac...  2.01 us
    ppermute x1, starting transfers between devices, per_device(): third = lax.ppermute(third, 'gy', near(gy))  1.84 us
    pallas_call x1, Pallas kernels, per_device(): pl.pallas_call(functools.partial(finish_kernel, gx, gy), in_specs=[on_chi...  1.27 us
    ppermute x1, waiting for transfers between devices, per_device(): fourth = lax.ppermute(fourth, 'gy', far(gy))  0.82 us
  transfers between devices with their start and end apart: 5, of which 2 were waited for; matrix products, arithmetic and copies ran while one was open for 0% of the time, Pallas kernels for 11%

profile of v5, /device:TPU:0, one launch (start us, length us, event | category | flops | bytes accessed | tf_op | source)
XLA Modules:
  0.0 19.4 jit_solution(15049809319896391631)
XLA Ops:
  0.6 2.0 %pack.1 = (f32[4,4,64,128]{3,2,1,0:T(8,128)S(1)}, f32[4,4,64,128]{3,2,1,0:T(8,128)S(1)}, f32[4,128]{1,0:T(4,128)S(1)}, s32[4,128]{1,0:T(4,128)S(1)}, f32[192,128...) custom-call(f32[4,4,64,128]{3,2,1,0:T(8,128)} %bitcast.15, ...), custom_call_target="tpu_custom_call" | custom-call | tf_op jit(solution)/shard_map/pack/pallas_call | solution.py:514
  2.6 0.5 %collective-permute-start = (f32[192,128]{1,0:T(8,128)S(1)}, f32[192,128]{1,0:T(8,128)S(1)}, u32[]{:S(2)}, u32[]{:S(2)}) collective-permute-start(f32[192,128]{1,0:T(8,128)S(1)} %get-tuple-element.27), channel_id=1, source_target_pairs={{0,4},{4,0},{8,12},{12,8},{16,20},{20,16},{24,28},{28,24},{1,5},{5... | collective-permute-start | bytes 294920 | tf_op jit(solution)/shard_map/ppermute | solution.py:545
  3.2 3.6 %collective-permute-start.1 = (f32[192,128]{1,0:T(8,128)S(1)}, f32[192,128]{1,0:T(8,128)S(1)}, u32[]{:S(2)}, u32[]{:S(2)}) collective-permute-start(f32[192,128]{1,0:T(8,128)S(1)} %get-tuple-element.28), channel_id=1, source_target_pairs={{0,28},{4,8},{8,4},{12,16},{16,12},{20,24},{24,20},{28,0},{1,29},{... | collective-permute-start | bytes 294920 | tf_op jit(solution)/shard_map/ppermute | solution.py:546
  6.7 4.0 %all-to-all-start = ((f32[32,5,1,128]{3,2,1,0:T(1,128)}), f32[32,5,1,128]{3,2,1,0:T(1,128)S(1)}, u32[]{:S(2)}, u32[]{:S(2)}) async-start(f32[32,5,1,128]{3,2,1,0:T(1,128)} %bitcast.17), calls=%async_computation | async-start | bytes 163840 | tf_op jit(solution)/shard_map/all_to_all | solution.py:547
  10.7 1.8 %collective-permute-start.2 = (f32[8,128]{1,0:T(8,128)S(1)}, f32[8,128]{1,0:T(8,128)S(1)}, u32[]{:S(2)}, u32[]{:S(2)}) collective-permute-start(f32[8,128]{1,0:T(8,128)S(1)} %get-tuple-element.33), channel_id=1, source_target_pairs={{0,1},{1,0},{2,3},{3,2},{4,5},{5,4},{6,7},{7,6},{8,9},{9,8},{10,11... | collective-permute-start | bytes 12296 | tf_op jit(solution)/shard_map/ppermute | solution.py:550
  12.5 2.4 %collective-permute-start.3 = (f32[8,128]{1,0:T(8,128)S(1)}, f32[8,128]{1,0:T(8,128)S(1)}, u32[]{:S(2)}, u32[]{:S(2)}) collective-permute-start(f32[8,128]{1,0:T(8,128)S(1)} %get-tuple-element.34), channel_id=1, source_target_pairs={{0,3},{1,2},{2,1},{3,0},{4,7},{5,6},{6,5},{7,4},{8,11},{9,10},{10,... | collective-permute-start | bytes 12296 | tf_op jit(solution)/shard_map/ppermute | solution.py:551
  14.9 0.0 collective-permute-done.first
  14.9 0.0 collective-permute-done.1.second
  14.9 2.2 %interior.1 = (f32[4,4,64,128]{3,2,1,0:T(8,128)S(1)}, f32[4,4,64,128]{3,2,1,0:T(8,128)S(1)}, f32[4,4,64,128]{3,2,1,0:T(8,128)S(1)}, f32[4,4,64,128]{3,2,1,0:T(8,...) custom-call(f32[4,4,64,128]{3,2,1,0:T(8,128)S(1)} %get-tuple-element.23.st, ...), custom_call_target="tpu_custom_call" | custom-call | flops 30000001024 | bytes 2400000 | tf_op jit(solution)/shard_map/interior/pallas_call | solution.py:553
  17.1 0.0 collective-permute-done.2.third
  17.1 0.8 %collective-permute-done.3.fourth = f32[8,128]{1,0:T(8,128)S(1)} collective-permute-done((f32[8,128]{1,0:T(8,128)S(1)}, f32[8,128]{1,0:T(8,128)S(1)}, u32[]{:S(2)}, u32[]{:S(2)}) %collective-permute-start.3) | collective-permute-done | bytes 4128 | tf_op jit(solution)/shard_map/ppermute | solution.py:551
  17.9 0.2 all-to-all-done
  18.1 1.3 %finish.1 = (f32[4,4,64,128]{3,2,1,0:T(8,128)}, f32[4,4,64,128]{3,2,1,0:T(8,128)}, f32[4,4,64,128]{3,2,1,0:T(8,128)}, f32[4,128]{1,0:T(4,128)}) custom-call(f32[4,4,64,128]{3,2,1,0:T(8,128)S(1)} %get-tuple-element.23.st, f32[4,4,64,128]{3,2,1,0:T(8,128)S(1)} %get-tuple-element.24.ct, ...), custom_call_target="tpu_custom_call", output_to_operand_aliasing={{0}: (10, {}), {1}: (11, {}), {2}: (12, {})} | custom-call | tf_op jit(solution)/shard_map/finish/pallas_call | solution.py:565
Async XLA Ops:
  2.6 12.3 %collective-permute-start = (f32[192,128]{1,0:T(8,128)S(1)}, f32[192,128]{1,0:T(8,128)S(1)}, u32[]{:S(2)}, u32[]{:S(2)}) collective-permute-start(f32[192,128]{1,0:T(8,128)S(1)} %get-tuple-element.27), channel_id=1, source_target_pairs={{0,4},{4,0},{8,12},{12,8},{16,20},{20,16},{24,28},{28,24},{1,5},{5... | collective-permute-start | bytes 294920 | tf_op jit(solution)/shard_map/ppermute | solution.py:545
  3.2 11.7 %collective-permute-start.1 = (f32[192,128]{1,0:T(8,128)S(1)}, f32[192,128]{1,0:T(8,128)S(1)}, u32[]{:S(2)}, u32[]{:S(2)}) collective-permute-start(f32[192,128]{1,0:T(8,128)S(1)} %get-tuple-element.28), channel_id=1, source_target_pairs={{0,28},{4,8},{8,4},{12,16},{16,12},{20,24},{24,20},{28,0},{1,29},{... | collective-permute-start | bytes 294920 | tf_op jit(solution)/shard_map/ppermute | solution.py:546
  6.7 11.4 %all-to-all-start = ((f32[32,5,1,128]{3,2,1,0:T(1,128)}), f32[32,5,1,128]{3,2,1,0:T(1,128)S(1)}, u32[]{:S(2)}, u32[]{:S(2)}) async-start(f32[32,5,1,128]{3,2,1,0:T(1,128)} %bitcast.17), calls=%async_computation | async-start | bytes 163840 | tf_op jit(solution)/shard_map/all_to_all | solution.py:547
  10.7 6.4 %collective-permute-start.2 = (f32[8,128]{1,0:T(8,128)S(1)}, f32[8,128]{1,0:T(8,128)S(1)}, u32[]{:S(2)}, u32[]{:S(2)}) collective-permute-start(f32[8,128]{1,0:T(8,128)S(1)} %get-tuple-element.33), channel_id=1, source_target_pairs={{0,1},{1,0},{2,3},{3,2},{4,5},{5,4},{6,7},{7,6},{8,9},{9,8},{10,11... | collective-permute-start | bytes 12296 | tf_op jit(solution)/shard_map/ppermute | solution.py:550
  12.5 5.4 %collective-permute-start.3 = (f32[8,128]{1,0:T(8,128)S(1)}, f32[8,128]{1,0:T(8,128)S(1)}, u32[]{:S(2)}, u32[]{:S(2)}) collective-permute-start(f32[8,128]{1,0:T(8,128)S(1)} %get-tuple-element.34), channel_id=1, source_target_pairs={{0,3},{1,2},{2,1},{3,0},{4,7},{5,6},{6,5},{7,4},{8,11},{9,10},{10,... | collective-permute-start | bytes 12296 | tf_op jit(solution)/shard_map/ppermute | solution.py:551
